TPU v7x, 32 devices: a whole 2x2x4 slice. The times are simulated.
32 devices in a mesh: dp: 8 (over z, y), chan: 4 (over x, core).
Axes of the slice: x: 2, y: 2, z: 4, core: 2. Of those that a mesh axis runs over, the one named last changes fastest.
Arguments:
- hidden_in: bfloat16 [768, 32768], P('chan', 'dp'), may hold values from -6 to 6
- lengths_short: int32 [128], P('dp'), may hold values from 32 to 128, as said below
- lengths_long: int32 [32], P('dp'), may hold values from 128 to 512, as said below
- qkv_weight: bfloat16 [4, 192, 576], P('chan'), may hold values from -0.4375 to 0.4375
- qv_bias: float32 [4, 384], P('chan'), may hold values from -1.75 to 1.75
- out_weight: bfloat16 [768, 768], P('chan'), may hold values from -2 to 2
- mixer_bias: float32 [768], replicated, may hold values from -3 to 3
- first_gain: float32 [768], replicated, may hold values from 0.5 to 1.5
- first_shift: float32 [768], replicated, may hold values from -3 to 3
- up_weight: bfloat16 [192, 3072], P(None, 'chan'), may hold values from -0.4375 to 0.4375
- up_bias: float32 [3072], P('chan'), may hold values from -1.75 to 1.75
- down_weight: bfloat16 [192, 3072], P(None, 'chan'), may hold values from -0.21875 to 0.21875
- down_bias: float32 [768], replicated, may hold values from -3 to 3
- second_gain: float32 [768], replicated, may hold values from 0.5 to 1.5
- second_shift: float32 [768], replicated, may hold values from -3 to 3
- out_grad: bfloat16 [32768, 768], P(('dp', 'chan')), may hold values from -6 to 6
Outputs:
- layer_out: bfloat16 [32768, 768], P(('dp', 'chan'))
- grad_input: float32 [768, 32768], P('chan', 'dp')
- grad_qkv_weight: float32 [4, 192, 576], P('chan', None, 'dp')
- grad_qv_bias: float32 [4, 384], P('chan')
- grad_out_weight: float32 [768, 768], P('chan', 'dp')
- grad_mixer_bias: float32 [768], P(('dp', 'chan'))
- grad_first_gain: float32 [768], P(('dp', 'chan'))
- grad_first_shift: float32 [768], P(('dp', 'chan'))
- grad_up_weight: float32 [192, 3072], P('dp', 'chan')
- grad_up_bias: float32 [3072], P('chan')
- grad_down_weight: float32 [192, 3072], P('dp', 'chan')
- grad_down_bias: float32 [768], P(('dp', 'chan'))
- grad_second_gain: float32 [768], P(('dp', 'chan'))
- grad_second_shift: float32 [768], P(('dp', 'chan'))
Inputs may be any that keep to these rules, and one draw needn't show every extreme that they name: `lengths_short`: tokens of a short sequence at positions under its length are valid keys; at least one short sequence has all 128 valid. `lengths_long`: likewise for the long sequences; at least one has all 512 valid.
All inputs are finite; a program needn't handle non-finite values.
Results may differ from a plain program's by a relative error of at most 0.017.
Values may be sent and summed in bfloat16 or wider, within the bound.
No kernel may reach another device: no remote copies, remote signals or barrier semaphores. Data moves between devices by JAX's collectives and lax.ppermute only.
A program may use at most 192 MiB of HBM per device.

v0:
```python
import functools

import jax
import jax.numpy as jnp
from jax import lax
from jax.experimental import pallas as pl
from jax.experimental.pallas import tpu as pltpu
from jax.sharding import PartitionSpec as P

HD = 64
LS = 128
LL = 512
TILE = 256
EPSILON = 1e-06
LOG2E = 1.4426950408889634
F32 = jnp.float32
BF16 = jnp.bfloat16
VMEM_LIMIT = 67043328
VMEM_SMALL = 8388608


def COST(us):
    return pl.CostEstimate(
        flops=int(us * 1.0e9), bytes_accessed=int(us * 1.0e6), transcendentals=0
    )


def dot(a, b, ca, cb):
    return lax.dot_general(a, b, (((ca,), (cb,)), ((), ())), preferred_element_type=F32)


def gelu_parts(v):
    av = jnp.abs(v)
    t = 1.0 / (1.0 + (0.3275911 * 0.7071067811865476) * av)
    e = jnp.exp2((-0.5 * LOG2E) * (v * v))
    poly = t * (
        0.5 * 0.254829592
        + t
        * (
            0.5 * -0.284496736
            + t * (0.5 * 1.421413741 + t * (0.5 * -1.453152027 + t * (0.5 * 1.061405429)))
        )
    )
    tail = poly * e
    phi = jnp.where(v >= 0, 1.0 - tail, tail)
    return phi, phi + v * (0.3989422804014327 * e)


def score_operands(heads, span, seq_len, lens, first, q, key, qa, ka):
    width = heads * HD
    scaled = q.astype(F32) * (HD**-0.5 * LOG2E)
    high = scaled.astype(BF16)
    low = (scaled - high.astype(F32)).astype(BF16)
    pos = lax.broadcasted_iota(jnp.int32, (16, seq_len), 1)
    row = lax.broadcasted_iota(jnp.int32, (16, seq_len), 0)
    for h in range(heads):
        rows = slice(h * HD, (h + 1) * HD)
        qa[h, 0:HD, :] = high[rows]
        qa[h, HD : 2 * HD, :] = low[rows]
        ka[h, 0:HD, :] = key[rows]
        ka[h, HD : 2 * HD, :] = key[rows]
    for i in range(span // seq_len):
        bad = (row == 0) & (pos >= lens[first + i])
        mask = jnp.where(bad, -1e9, 0.0).astype(BF16)
        for h in range(heads):
            ka[h, 2 * HD :, i * seq_len : (i + 1) * seq_len] = mask


def one_rows(qa):
    row = lax.broadcasted_iota(jnp.int32, (16, qa.shape[2]), 0)
    ones = jnp.where(row == 0, 1.0, 0.0).astype(BF16)
    for h in range(qa.shape[0]):
        qa[h, 2 * HD :, :] = ones


def slot_block(me, s):
    return lax.bitwise_xor(me[0], lax.bitwise_and(s, 3)) * 2 + lax.shift_right_logical(s, 2)


def attn_fwd_kernel(heads, short_blocks, me, lens_s, lens_l, x, w, b, proj, *refs):
    outs = refs[:8]
    lse, scr, qa, ka, bcol = refs[8:]
    k = pl.program_id(0)
    block = slot_block(me, k)
    width = heads * HD
    span = x.shape[1]

    @pl.when(k == 0)
    def _():
        t = jnp.broadcast_to(b[...], (8, 2 * width)).T
        bcol[:width] = t[:width]
        bcol[width : 2 * width] = jnp.zeros((width, 8), F32)
        bcol[2 * width :] = t[width:]
        one_rows(qa)

    proj[0] = (dot(w[...], x[...], 0, 0) + bcol[:, 0:1]).astype(BF16)

    def run(seq_len, lens, first):
        score_operands(
            heads, span, seq_len, lens, first, proj[0, :width], proj[0, width : 2 * width], qa, ka
        )
        items = [(i, h) for i in range(span // seq_len) for h in range(heads)]

        def score(i, h):
            cols = slice(i * seq_len, (i + 1) * seq_len)
            return dot(ka[h, :, cols], qa[h, :, cols], 0, 0)

        s = score(*items[0])
        for n, (i, h) in enumerate(items):
            later = score(*items[n + 1]) if n + 1 < len(items) else None
            cols = slice(i * seq_len, (i + 1) * seq_len)
            m = jnp.max(s, axis=0, keepdims=True)
            e = jnp.exp2(s - m)
            total = jnp.sum(e, axis=0, keepdims=True)
            val = proj[0, 2 * width + h * HD : 2 * width + (h + 1) * HD, cols]
            c = dot(val, e.astype(BF16), 1, 0) * (1.0 / total)
            scr[h * HD : (h + 1) * HD, cols] = c.astype(BF16)
            lse[0, h : h + 1, cols] = m + jnp.log2(total)
            s = later

    @pl.when(block < short_blocks)
    def _():
        run(LS, lens_s, block * (span // LS))

    @pl.when(block >= short_blocks)
    def _():
        run(LL, lens_l, (block - short_blocks) * (span // LL))

    for i, out in enumerate(outs):

        @pl.when(k == i)
        def _():
            out[0] = scr[...]
            if i % 4:
                out[1] = x[...]


def attn_fwd(me, lens_s, lens_l, x, w, b):
    width, tokens = x.shape
    span = tokens // 8
    heads = width // HD
    short_blocks = lens_s.shape[0] * LS // span
    fixed = lambda k, *_: (0, 0)
    parts = [(2 if k % 4 else 1, width, span) for k in range(8)]
    return pl.pallas_call(
        functools.partial(attn_fwd_kernel, heads, short_blocks),
        grid_spec=pltpu.PrefetchScalarGridSpec(
            num_scalar_prefetch=3,
            grid=(8,),
            in_specs=[
                pl.BlockSpec((width, span), lambda k, me, *_: (0, slot_block(me, k))),
                pl.BlockSpec(w.shape, fixed),
                pl.BlockSpec(b.shape, fixed),
            ],
            out_specs=[
                pl.BlockSpec((1, 3 * width, span), lambda k, *_: (k, 0, 0)),
                *[pl.BlockSpec(part, lambda k, *_: (0, 0, 0)) for part in parts],
                pl.BlockSpec((1, heads, span), lambda k, *_: (k, 0, 0)),
            ],
            scratch_shapes=[
                pltpu.VMEM((width, span), BF16),
                pltpu.VMEM((heads, 2 * HD + 16, span), BF16),
                pltpu.VMEM((heads, 2 * HD + 16, span), BF16),
                pltpu.VMEM((3 * width, 8), F32),
            ],
        ),
        out_shape=[
            jax.ShapeDtypeStruct((8, 3 * width, span), BF16),
            *[jax.ShapeDtypeStruct(part, BF16) for part in parts],
            jax.ShapeDtypeStruct((8, heads, span), F32),
        ],
        cost_estimate=COST(16.0),
        compiler_params=pltpu.CompilerParams(vmem_limit_bytes=VMEM_LIMIT),
        name="attn_fwd",
    )(me, lens_s, lens_l, x, w, b)


def attn_bwd_kernel(first, count, heads, short_blocks, first_call, split, *refs):
    me, parity, lens_s, lens_l, x, w, proj, lse = refs[:8]
    gs = refs[8 : 8 + count]
    refs = refs[8 + count :]
    if not first_call:
        acc_in, bias_in = refs[:2]
        refs = refs[3:]
    gin = refs[0]
    if split == 0:
        acc, bias = refs[1:3]
        refs = refs[3:]
    elif split == 1:
        out, bias = refs[1:3]
        acc = refs[-1]
        refs = refs[3:-1]
    else:
        keep, send, extra = refs[1:4]
        bias, acc = refs[-2:]
        refs = refs[4:-2]
    dproj, gsc, qa, ka = refs
    step = pl.program_id(0)
    block = slot_block(me, first + step)
    width = heads * HD
    span = x.shape[1]
    scale = HD**-0.5

    @pl.when(step == 0)
    def _():
        one_rows(qa)

    for i, g in enumerate(gs):

        @pl.when(step == i)
        def _():
            gsc[...] = g[...]

    def run(seq_len, lens, first):
        score_operands(
            heads, span, seq_len, lens, first, proj[0, :width], proj[0, width : 2 * width], qa, ka
        )
        items = [(i, h) for i in range(span // seq_len) for h in range(heads)]

        def score(i, h):
            cols = slice(i * seq_len, (i + 1) * seq_len)
            val = proj[0, 2 * width + h * HD : 2 * width + (h + 1) * HD, cols]
            go = gsc[0, h * HD : (h + 1) * HD, cols]
            return dot(ka[h, :, cols], qa[h, :, cols], 0, 0), dot(val, go, 0, 0)

        pair = score(*items[0])
        for n, (i, h) in enumerate(items):
            later = score(*items[n + 1]) if n + 1 < len(items) else None
            cols = slice(i * seq_len, (i + 1) * seq_len)
            rq, rk, rv = [slice(j * width + h * HD, j * width + (h + 1) * HD) for j in range(3)]
            q = proj[0, rq, cols]
            key = proj[0, rk, cols]
            go = gsc[0, h * HD : (h + 1) * HD, cols]
            s, gp = pair
            p = jnp.exp2(s - lse[0, h : h + 1, cols])
            inner = jnp.sum(p * gp, axis=0, keepdims=True)
            g = (p * (gp - inner)).astype(BF16)
            dproj[rq, cols] = (dot(key, g, 1, 0) * scale).astype(BF16)
            dproj[rk, cols] = (dot(q, g, 1, 1) * scale).astype(BF16)
            dproj[rv, cols] = dot(go, p.astype(BF16), 1, 1).astype(BF16)
            pair = later

    @pl.when(block < short_blocks)
    def _():
        run(LS, lens_s, block * (span // LS))

    @pl.when(block >= short_blocks)
    def _():
        run(LL, lens_l, (block - short_blocks) * (span // LL))

    gin[...] = dot(w[...], dproj[...], 1, 0) + gsc[1].astype(F32)
    part = dot(dproj[...], x[...], 1, 1)
    sums = dot(jnp.ones((8, span), BF16), dproj[...], 1, 1)

    @pl.when(step == 0)
    def _():
        if first_call:
            acc[...] = part
            bias[...] = sums
        else:
            acc[...] = acc_in[...] + part
            bias[...] = bias_in[...] + sums

    @pl.when(step > 0)
    def _():
        acc[...] += part
        bias[...] += sums

    if split == 1:

        @pl.when(step == count - 1)
        def _():
            rows = out.shape[1]
            for d in range(out.shape[0]):
                out[d] = acc[d * rows : (d + 1) * rows, :].astype(BF16)

    if split == 2:

        @pl.when(step == count - 1)
        def _():
            pairs, rows = keep.shape[:2]
            mine = parity[0]
            for d in range(pairs):
                a = pl.ds(pl.multiple_of((2 * d + mine) * rows, 8), rows)
                c = pl.ds(pl.multiple_of((2 * d + 1 - mine) * rows, 8), rows)
                keep[d] = acc[a, :].astype(BF16)
                send[d] = acc[c, :].astype(BF16)
            total = jnp.concatenate(
                [bias[:, i * width : (i + 1) * width] for i in range(3)], axis=0
            )
            extra[...] = total
            high = total.astype(BF16)
            send[pairs, :24] = high
            send[pairs, 24:48] = (total - high.astype(F32)).astype(BF16)


def attn_bwd(
    first, count, me, parity, lens_s, lens_l, x, w, proj, lse, g, carry, dp_count, split
):
    width, tokens = x.shape
    span = tokens // 8
    heads = width // HD
    short_blocks = lens_s.shape[0] * LS // span
    fixed = lambda k, *_: (0, 0)
    fixed3 = lambda k, *_: (0, 0, 0)
    here = lambda k, me, *_: (0, slot_block(me, first + k))
    slot = lambda k, *_: (first + k, 0, 0)
    first_call = carry is None
    acc_spec = pl.BlockSpec((3 * width, width), fixed)
    bias_spec = pl.BlockSpec((8, 3 * width), fixed)
    acc_shape = jax.ShapeDtypeStruct((3 * width, width), F32)
    bias_shape = jax.ShapeDtypeStruct((8, 3 * width), F32)
    mine = g[first : first + count]
    in_specs = [
        pl.BlockSpec((width, span), here),
        pl.BlockSpec(w.shape, fixed),
        pl.BlockSpec((1, 3 * width, span), slot),
        pl.BlockSpec((1, heads, span), slot),
    ] + [pl.BlockSpec((2, width, span), fixed3)] * len(mine)
    args = [x, w, proj, lse, *mine]
    aliases = {}
    if not first_call:
        gin, acc, bias = carry
        in_specs += [acc_spec, bias_spec, pl.BlockSpec(memory_space=pl.ANY)]
        args += [acc, bias, gin]
        aliases = {4 + len(args) - 1: 0}
    rows = 3 * width // dp_count
    scratch = []
    if split == 0:
        tail = [(acc_spec, acc_shape), (bias_spec, bias_shape)]
    elif split == 1:
        shape = (dp_count, rows, width)
        tail = [
            (pl.BlockSpec(shape, fixed3), jax.ShapeDtypeStruct(shape, BF16)),
            (bias_spec, bias_shape),
        ]
        scratch = [pltpu.VMEM(acc_shape.shape, F32)]
    else:
        keep = (dp_count // 2, rows, width)
        send = (dp_count // 2 + 1, rows, width)
        tail = [
            (pl.BlockSpec(keep, fixed3), jax.ShapeDtypeStruct(keep, BF16)),
            (pl.BlockSpec(send, fixed3), jax.ShapeDtypeStruct(send, BF16)),
            (pl.BlockSpec((24, width), fixed), jax.ShapeDtypeStruct((24, width), F32)),
        ]
        scratch = [pltpu.VMEM(bias_shape.shape, F32), pltpu.VMEM(acc_shape.shape, F32)]
    return pl.pallas_call(
        functools.partial(
            attn_bwd_kernel, first, count, heads, short_blocks, first_call, split
        ),
        grid_spec=pltpu.PrefetchScalarGridSpec(
            num_scalar_prefetch=4,
            grid=(count,),
            in_specs=in_specs,
            out_specs=[pl.BlockSpec((width, span), here)] + [t[0] for t in tail],
            scratch_shapes=[
                pltpu.VMEM((3 * width, span), BF16),
                pltpu.VMEM((2, width, span), BF16),
                pltpu.VMEM((heads, 2 * HD + 16, span), BF16),
                pltpu.VMEM((heads, 2 * HD + 16, span), BF16),
            ]
            + scratch,
        ),
        out_shape=[jax.ShapeDtypeStruct((width, tokens), F32)] + [t[1] for t in tail],
        input_output_aliases=aliases,
        cost_estimate=COST(4.0 * count),
        compiler_params=pltpu.CompilerParams(vmem_limit_bytes=VMEM_LIMIT),
        name=f"attn_bwd{first}",
    )(me, parity, lens_s, lens_l, *args)


def prep_kernel(w0, w1, w2, w3, *refs):
    params = refs[:6]
    owt, upt, dnt, upn, dnn, ub, cols, ow = refs[6:]
    weights = (w0, w1, w2, w3)
    model = owt.shape[0]
    width = model // 4

    def eye(n):
        a = lax.broadcasted_iota(jnp.int32, (n, n), 0)
        b = lax.broadcasted_iota(jnp.int32, (n, n), 1)
        return jnp.where(a == b, 1.0, 0.0).astype(BF16)

    big, small = eye(256), eye(width)
    for k, w in enumerate(weights):
        ks = slice(k * width, (k + 1) * width)
        ow[ks, :] = w[:width, :]
        for at in range(0, model, 256):
            lanes = slice(at, at + 256)
            for ref, first in ((upt, width), (dnt, 2 * width)):
                t = dot(big, w[first : first + width, lanes], 1, 1).astype(BF16)
                for g in range(4):
                    low, high = max(at, g * width), min(at + 256, (g + 1) * width)
                    if low < high:
                        start = k * width + low - g * width
                        ref[g, start : start + high - low, :] = t[low - at : high - at, :]
        bt = w[3 * width :, :].astype(F32).T
        ub[:, k : k + 1] = (bt[:, 2:3] + bt[:, 1:2]) + bt[:, 0:1]

    @pl.loop(0, model // 256)
    def _(i):
        at = pl.ds(pl.multiple_of(i * 256, 256), 256)
        owt[at, :] = dot(big, ow[:, at], 1, 1).astype(BF16)

    @pl.loop(0, 4)
    def _(g):
        upn[g] = dot(small, upt[g], 1, 1).astype(BF16)
        dnn[g] = dot(small, dnt[g], 1, 1).astype(BF16)

    for j, p in enumerate(params):
        cols[:, j : j + 1] = jnp.broadcast_to(p[...].reshape(1, model), (8, model)).T[:, 0:1]


def prep(weights, params):
    model = weights[0].shape[1]
    width = model // 4
    vmem = pl.BlockSpec(memory_space=pltpu.VMEM)
    shapes = [
        jax.ShapeDtypeStruct((model, model), BF16),
        jax.ShapeDtypeStruct((4, model, width), BF16),
        jax.ShapeDtypeStruct((4, model, width), BF16),
        jax.ShapeDtypeStruct((4, width, model), BF16),
        jax.ShapeDtypeStruct((4, width, model), BF16),
        jax.ShapeDtypeStruct((model, 8), F32),
        jax.ShapeDtypeStruct((model, 8), F32),
        jax.ShapeDtypeStruct((model, model), BF16),
    ]
    return pl.pallas_call(
        prep_kernel,
        in_specs=[vmem] * 10,
        out_specs=[vmem] * len(shapes),
        out_shape=shapes,
        cost_estimate=COST(4.0),
        compiler_params=pltpu.CompilerParams(vmem_limit_bytes=VMEM_LIMIT),
        name="prep",
    )(*weights, *params)


def mid_kernel(half, width, blocks, me, *refs):
    ctx, hid = refs[0:4], refs[4:8]
    og, ub, cols = refs[8:11]
    given = refs[11:17]
    at = 17
    if half:
        acc_hbm, vec_in = refs[at : at + 3], refs[at + 3]
        at += 5
    lo = refs[at]
    back = refs[at + 1 : at + 5]
    at += 5
    if half:
        keep, send, vec_out = refs[at : at + 3]
        at += 3
    else:
        acc_hbm, vec = refs[at : at + 3], refs[at + 3]
        at += 4
    (gow, gup, gdn, owt, upt, dnt, upn, dnn, ow) = refs[at : at + 9]
    at += 9
    (sums, act, slope, first, n1s, gps_s, cats, lows, sem, acc_sem) = refs[at : at + 10]
    if half:
        vec = refs[at + 10]
    accs = (gow, gup, gdn)
    step = pl.program_id(0)
    last = pl.num_programs(0) - 1
    model = 4 * width
    inv = 1.0 / model
    held = (owt, upt, dnn, dnt, upn, ow)

    def own(k):
        return pl.ds(pl.multiple_of(lax.bitwise_xor(me[0], k) * width, width), width)

    def fetch(i):
        return pltpu.make_async_copy(given[i], held[i], sem.at[i])

    def ready(i):
        @pl.when(step == 0)
        def _():
            fetch(i).wait()

    def acc_copy(i):
        if half:
            return pltpu.make_async_copy(acc_hbm[i], accs[i], acc_sem.at[i])
        return pltpu.make_async_copy(accs[i], acc_hbm[i], acc_sem.at[i])

    @pl.when(step == 0)
    def _():
        for i in range(6):
            fetch(i).start()
        if half:
            for i in range(3):
                acc_copy(i).start()
        row = lax.broadcasted_iota(jnp.int32, (16, TILE), 0)
        for g in range(4):
            lows[g, width:, :] = jnp.where(row == 0, 1.0, 0.0).astype(BF16)
        sums[...] = jnp.zeros_like(sums)

    def before(value):
        return value if half else jnp.where(step == 0, 0.0, value)

    def acc_ready(i):
        if half:

            @pl.when(step == 0)
            def _():
                acc_copy(i).wait()

    def acc_done(i):
        if not half:

            @pl.when(step == last)
            def _():
                acc_copy(i).start()

    def col(j):
        return cols[:, j : j + 1]

    def add_sum(j, value):
        sums[j] += sum(value[:, i : i + 128] for i in range(0, TILE, 128))

    for k in range(4):
        cats[k * width : (k + 1) * width, :] = ctx[k][0]
    ready(0)
    first[...] = dot(owt[...], cats[...], 1, 0) + col(0)
    for k in range(4):
        first[own(k), :] += hid[k][...].reshape(width, TILE).astype(F32)
    pre = first[...]
    cen = pre - jnp.sum(pre, axis=0, keepdims=True) * inv
    r1 = lax.rsqrt(jnp.sum(cen * cen, axis=0, keepdims=True) * inv + EPSILON)
    n1 = cen * r1
    n1s[...] = n1
    normed = n1 * col(1) + col(2)
    first[...] = normed
    low = normed.astype(BF16)
    for g in range(4):
        lows[g, :width, :] = low[g * width : (g + 1) * width, :]
    ready(1)
    ready(2)

    def pre_act(g):
        return dot(upt[g], lows[g, :width, :], 1, 0)

    later = pre_act(0)
    for g in range(4):
        rows = slice(g * width, (g + 1) * width)
        raw = later
        if g < 3:
            later = pre_act(g + 1)
        for k in range(4):
            units = slice(k * width, (k + 1) * width)
            pa = raw[units, :] + ub[rows, k : k + 1]
            phi, sl = gelu_parts(pa)
            act[g, units, :] = (pa * phi).astype(BF16)
            slope[g, units, :] = sl
        first[rows, :] += dot(dnn[g], act[g], 1, 0) + cols[rows, 3:4]
    pre = first[...]
    cen = pre - jnp.sum(pre, axis=0, keepdims=True) * inv
    r2 = lax.rsqrt(jnp.sum(cen * cen, axis=0, keepdims=True) * inv + EPSILON)
    n2 = cen * r2
    lo[...] = (n2 * col(4) + col(5)).astype(BF16).T
    ogt = og[...].T.astype(F32)
    add_sum(4, ogt * n2)
    add_sum(5, ogt)
    u = ogt * col(4)
    gps = r2 * (
        u
        - jnp.sum(u, axis=0, keepdims=True) * inv
        - n2 * (jnp.sum(u * n2, axis=0, keepdims=True) * inv)
    )
    add_sum(3, gps)
    gdl = gps.astype(BF16)
    gps_s[...] = gps
    ready(3)
    ready(4)
    acc_ready(1)
    acc_ready(2)

    def grad_act(g):
        return dot(dnt[g], gdl[g * width : (g + 1) * width, :], 1, 0)

    later = grad_act(0)
    for g in range(4):
        rows = slice(g * width, (g + 1) * width)
        raw = later
        if g < 3:
            later = grad_act(g + 1)
        gdn[g] = before(gdn[g]) + dot(act[g], gdl[rows, :], 1, 1)
        gpa = (raw * slope[g]).astype(BF16)
        gup[g] = before(gup[g]) + dot(gpa, lows[g], 1, 1)
        gps_s[rows, :] += dot(upn[g], gpa, 1, 0)
    acc_done(1)
    acc_done(2)
    gn = gps_s[...]
    n1 = n1s[...]
    add_sum(1, gn * n1)
    add_sum(2, gn)
    u = gn * col(1)
    gpf = r1 * (
        u
        - jnp.sum(u, axis=0, keepdims=True) * inv
        - n1 * (jnp.sum(u * n1, axis=0, keepdims=True) * inv)
    )
    gpl = gpf.astype(BF16)
    first[...] = gpl.astype(F32)
    add_sum(0, first[...])
    ready(5)
    acc_ready(0)
    gow[...] = before(gow[...]) + dot(gpl, cats[...], 1, 1)
    acc_done(0)
    for k in range(4):
        back[k][1] = first[own(k), :].astype(BF16)
        back[k][0] = dot(ow[k * width : (k + 1) * width, :], gpl, 1, 0).astype(BF16)

    @pl.when(step == last)
    def _():
        lane = lax.broadcasted_iota(jnp.int32, (1, 128), 1)
        total = vec_in[...] if half else jnp.zeros((model, 128), F32)
        for j in range(6):
            total += jnp.where(lane == j, jnp.sum(sums[j], axis=1, keepdims=True), 0.0)
        vec[...] = total
        if half:
            for g in range(4):
                for k in range(4):
                    vec[own(k), :] += jnp.where(
                        lane == 6 + g, gup[g, k * width : (k + 1) * width, width : width + 1], 0.0
                    )
            more = vec[...].T[:16]
            vec_out[...] = more
            part = width // blocks

            @pl.loop(0, 2)
            def _(far):
                for near in range(2):
                    dest = send if near else keep
                    units = pl.ds(pl.multiple_of((2 * far + near) * width, 8), width)
                    up_rows = pl.ds(pl.multiple_of(far * 3 * width, 16), width)
                    down_rows = pl.ds(pl.multiple_of((far * 3 + 1) * width, 16), width)
                    for g in range(4):
                        lanes = slice(g * width, (g + 1) * width)
                        dest[up_rows, lanes] = gup[g, units, :width].T.astype(BF16)
                        dest[down_rows, lanes] = gdn[g, units, :].T.astype(BF16)

            pairs = 2 if blocks > 1 else 1

            @pl.loop(0, blocks // pairs)
            def _(pair):
                for k in range(4):
                    dest = send if k % 2 else keep
                    base = ((k // 2) * 3 + 2) * width
                    units = slice(k * width, (k + 1) * width)
                    to = pl.ds(pl.multiple_of(base + pair * pairs * part, 16), pairs * part)
                    for g in range(4):
                        lanes = slice(g * width, (g + 1) * width)
                        rows = []
                        for i in range(pairs):
                            start = ((pair * pairs + i) * 4 + g) * part
                            rows.append(gow[pl.ds(pl.multiple_of(start, 8), part), units])
                        dest[to, lanes] = jnp.concatenate(rows, axis=0).astype(BF16)

            if blocks > 1:
                high = more.astype(BF16)
                send[6 * width : 6 * width + 16, :] = high
                send[6 * width + part : 6 * width + part + 16, :] = (
                    more - high.astype(F32)
                ).astype(BF16)
        else:
            for i in range(3):
                acc_copy(i).wait()


def mid(half, me, ctx, hid, og, ready, carry, blocks):
    width, span = ctx[0].shape[1:]
    model = 4 * width
    steps = span // TILE
    whole2 = lambda i, *_: (0, 0)
    ctx_tile = pl.BlockSpec((1, width, TILE), lambda i, *_: (0, 0, i))
    hid_own = pl.BlockSpec((width, TILE), lambda i, me: (0, (me[0] * 2 + half) * steps + i))
    hid_tile = pl.BlockSpec((1, width, TILE), lambda i, *_: (1, 0, i))
    back_tile = pl.BlockSpec((2, width, TILE), lambda i, *_: (0, 0, i))
    row_in = pl.BlockSpec((TILE, model), lambda i, *_: (half * steps + i, 0))
    hbm = pl.BlockSpec(memory_space=pl.ANY)
    column = pl.BlockSpec((model, 8), whole2)
    vec_spec = pl.BlockSpec((model, 128), whole2)
    owt, upt, dnt, upn, dnn, ub, cols, ow = ready
    in_specs = [ctx_tile] * 4 + [hid_own] + [hid_tile] * 3 + [row_in, column, column] + [hbm] * 6
    args = [*ctx, *hid, og, ub, cols, owt, upt, dnn, dnt, upn, ow]
    accs = [(model, model), (4, model, width + 16), (4, model, width)]
    piece = jax.ShapeDtypeStruct((2, width, span), BF16)
    scratch = [pltpu.VMEM(a, F32) for a in accs] + [
        pltpu.VMEM((model, model), BF16),
        pltpu.VMEM((4, model, width), BF16),
        pltpu.VMEM((4, model, width), BF16),
        pltpu.VMEM((4, width, model), BF16),
        pltpu.VMEM((4, width, model), BF16),
        pltpu.VMEM((model, model), BF16),
        pltpu.VMEM((6, model, 128), F32),
        pltpu.VMEM((4, model, TILE), BF16),
        pltpu.VMEM((4, model, TILE), F32),
        pltpu.VMEM((model, TILE), F32),
        pltpu.VMEM((model, TILE), F32),
        pltpu.VMEM((model, TILE), F32),
        pltpu.VMEM((model, TILE), BF16),
        pltpu.VMEM((4, width + 16, TILE), BF16),
        pltpu.SemaphoreType.DMA((6,)),
        pltpu.SemaphoreType.DMA((3,)),
    ]
    aliases = {}
    if half:
        in_specs += [hbm] * 3 + [vec_spec, hbm]
        aliases = {len(args) + 5: 0}
        args += list(carry)
        extra = 2 * (width // blocks) if blocks > 1 else 0
        rows = [6 * width, 6 * width + extra]
        tail_specs = [pl.BlockSpec((r, model), whole2) for r in rows + [16]]
        tail_shapes = [jax.ShapeDtypeStruct((r, model), BF16) for r in rows]
        tail_shapes += [jax.ShapeDtypeStruct((16, model), F32)]
        scratch += [pltpu.VMEM((model, 128), F32)]
    else:
        tail_specs = [hbm] * 3 + [vec_spec]
        tail_shapes = [jax.ShapeDtypeStruct(a, F32) for a in accs + [(model, 128)]]
    return pl.pallas_call(
        functools.partial(mid_kernel, half, width, blocks),
        grid_spec=pltpu.PrefetchScalarGridSpec(
            num_scalar_prefetch=1,
            grid=(steps,),
            in_specs=in_specs,
            out_specs=[row_in] + [back_tile] * 4
            + tail_specs,
            scratch_shapes=scratch,
        ),
        out_shape=[jax.ShapeDtypeStruct((2 * span, model), BF16)] + [piece] * 4 + tail_shapes,
        input_output_aliases=aliases,
        cost_estimate=COST(25.0),
        compiler_params=pltpu.CompilerParams(vmem_limit_bytes=VMEM_LIMIT),
        name=f"mid{half}",
    )(me, *args)


def combine_kernel(size, outer, inner, index, keep, recv, extra, kept, sent, extra_out):
    rows = extra.shape[0]
    more = extra[...] + (recv[size, :rows].astype(F32) + recv[size + 1, :rows].astype(F32))
    extra_out[...] = more
    hi = more.astype(BF16)
    sent[size // 2, :rows] = hi
    sent[size // 2 + 1, :rows] = (more - hi.astype(F32)).astype(BF16)
    mine = index[0]
    for o in range(outer):
        a = pl.ds((o * 2 + mine) * inner, inner)
        b = pl.ds((o * 2 + 1 - mine) * inner, inner)
        c = slice(o * inner, (o + 1) * inner)
        kept[c] = (keep[a].astype(F32) + recv[a].astype(F32)).astype(BF16)
        sent[c] = (keep[b].astype(F32) + recv[b].astype(F32)).astype(BF16)


def combine(index, keep, recv, extra, outer, inner, name):
    size, rows, lanes = keep.shape
    vmem = pl.BlockSpec(memory_space=pltpu.VMEM)
    shapes = [
        jax.ShapeDtypeStruct((size // 2, rows, lanes), BF16),
        jax.ShapeDtypeStruct((size // 2 + 2, rows, lanes), BF16),
        jax.ShapeDtypeStruct(extra.shape, F32),
    ]
    return pl.pallas_call(
        functools.partial(combine_kernel, size, outer, inner),
        in_specs=[pl.BlockSpec(memory_space=pltpu.SMEM)] + [vmem] * 3,
        out_specs=[vmem] * len(shapes),
        out_shape=shapes,
        cost_estimate=COST(1.0),
        compiler_params=pltpu.CompilerParams(vmem_limit_bytes=VMEM_LIMIT),
        name=name,
    )(index, keep, recv, extra)


def blend_kernel(joint, last, index, wk, wr, vec, qk, *refs):
    if not joint:
        qr, qb, refs = refs[0], refs[1], refs[2:]
    nw, rows, model = wk.shape
    nq, width = qk.shape[0], qk.shape[2]
    pitch = model // 3
    if joint:
        terms = wr[nw].astype(F32)
        more = vec[:12] + (terms[:12] + terms[12:24])
    else:
        more = vec[:12] + (wr[nw, :16].astype(F32) + wr[nw + 1, :16].astype(F32))[:12]
        bias = qb[...] + (qr[nq, :24].astype(F32) + qr[nq, 24:48].astype(F32))

    def wsum(i):
        return wk[i].astype(F32) + wr[i].astype(F32)

    def qsum(i, j):
        part = slice(j * rows, (j + 1) * rows)
        if joint:
            other = wr[nw + 1 + i, :, j * pitch : j * pitch + width]
        else:
            other = qr[i, part, :]
        return qk[i, part, :].astype(F32) + other.astype(F32)

    if last:
        gup, gdn, gow, gqkv, gqv, gub = refs[:6]
        vecs = refs[6:]
        gup[...] = wsum(0)
        gdn[...] = wsum(1)
        ow = wsum(2)
        quarter = model // 4
        gow[...] = jnp.concatenate(
            [ow[:, j * quarter : (j + 1) * quarter] for j in range(4)], axis=0
        ).T
        for j in range(3):
            gqkv[j * rows : (j + 1) * rows, :] = qsum(0, j)
        gqv[:, :width] = more[10:11, :width]
        gqv[:, width:] = more[10:11, 2 * pitch : 2 * pitch + width]
        own = vecs[0].shape[0]
        more = jnp.concatenate([more, jnp.zeros((4, model), F32)], axis=0)
        here = pltpu.roll(more, index[1], 1)
        for j, v in enumerate(vecs):
            v[...] = here[j, :own]
        here = pltpu.roll(more, index[2], 1)
        gub[...] = jnp.concatenate([here[6 + j, :quarter] for j in range(4)])
        return
    wkept, sent, vec_out, qkept = refs
    mine = index[0]
    vec_out[:12] = more
    vec_out[12:] = jnp.zeros((4, model), F32)
    if not joint:
        for j in range(3):
            vec_out[10:11, j * pitch : j * pitch + width] = bias[8 * j : 8 * j + 1]
    half = nw // 2
    more = vec_out[:12]
    hi = more.astype(BF16).astype(F32)
    sent[half, :24] = jnp.concatenate([hi, more - hi], axis=0).astype(BF16)
    for i in range(half):
        wkept[i] = wsum(2 * i + mine).astype(BF16)
        sent[i] = wsum(2 * i + 1 - mine).astype(BF16)
    at = half + 1
    for i in range(nq // 2):
        for j in range(3):
            qkept[i, j * rows : (j + 1) * rows, :] = qsum(2 * i + mine, j).astype(BF16)
            sent[at + i, :, j * pitch : j * pitch + width] = qsum(2 * i + 1 - mine, j).astype(BF16)


def blend(index, wk, wr, vec, qk, qr, qb, last, name):
    nw, rows, model = wk.shape
    nq, _, width = qk.shape
    vmem = pl.BlockSpec(memory_space=pltpu.VMEM)
    args = [wk, wr, vec, qk] + ([] if qr is None else [qr, qb])
    shape = jax.ShapeDtypeStruct
    if last:
        quarter = model // 4
        shapes = [
            shape((rows, model), F32),
            shape((rows, model), F32),
            shape((quarter, 4 * rows), F32),
            shape((3 * rows, width), F32),
            shape((1, 2 * width), F32),
            shape((model,), F32),
        ] + [shape((rows,), F32)] * 6
    else:
        shapes = [
            shape((nw // 2, rows, model), BF16),
            shape((nw // 2 + nq // 2 + 1, rows, model), BF16),
            shape(vec.shape, F32),
            shape((nq // 2, 3 * rows, width), BF16),
        ]
    return pl.pallas_call(
        functools.partial(blend_kernel, qr is None, last),
        in_specs=[pl.BlockSpec(memory_space=pltpu.SMEM)] + [vmem] * len(args),
        out_specs=[vmem] * len(shapes),
        out_shape=shapes,
        cost_estimate=COST(1.0),
        compiler_params=pltpu.CompilerParams(vmem_limit_bytes=VMEM_SMALL),
        name=name,
    )(index, *args)


def swap(value, axis, bit):
    count = lax.axis_size(axis)
    return lax.ppermute(value, axis, [(i, i ^ bit) for i in range(count)])


def to_chan(pieces):
    return [pieces[0]] + [swap(pieces[k], "chan", k) for k in range(1, 4)]


def gather_chan(value):
    near = swap(value, "chan", 1)
    far = swap(value, "chan", 2)
    return [value, near, far, swap(far, "chan", 1)]


def scatter_dp(pieces):
    index = lax.axis_index("dp")
    count, bit = pieces.shape[0], 1
    while count > 1:
        view = pieces.reshape((count // 2, 2) + pieces.shape[1:])
        digit = (index // bit) % 2
        mine = lax.dynamic_index_in_dim(view, digit, 1, keepdims=False).astype(F32)
        other = lax.dynamic_index_in_dim(view, 1 - digit, 1, keepdims=False)
        total = mine + swap(other, "dp", bit).astype(F32)
        count, bit = count // 2, bit * 2
        pieces = total if count == 1 else total.astype(pieces.dtype)
    return pieces[0]


def sum_dp(value):
    bit = 1
    while bit < lax.axis_size("dp"):
        value = value + swap(value, "dp", bit)
        bit *= 2
    return value


def pack_kernel(ow, up, dn, ub, weights):
    width = ow.shape[0]
    for i, w in enumerate((ow, up, dn)):
        weights[i * width : (i + 1) * width, :] = w[...]
    whole = jnp.broadcast_to(ub[...].reshape(1, -1), (16, ub.shape[0]))
    high = whole.astype(BF16)
    rest = whole - high.astype(F32)
    middle = rest.astype(BF16)
    low = (rest - middle.astype(F32)).astype(BF16)
    row = lax.broadcasted_iota(jnp.int32, whole.shape, 0)
    terms = jnp.where(
        row == 0,
        high.astype(F32),
        jnp.where(row == 1, middle.astype(F32), low.astype(F32)),
    )
    weights[3 * width :, :] = terms.astype(BF16)


def pack(ow, up, dn, ub):
    width, model = ow.shape
    vmem = pl.BlockSpec(memory_space=pltpu.VMEM)
    return pl.pallas_call(
        pack_kernel,
        in_specs=[vmem] * 4,
        out_specs=vmem,
        out_shape=jax.ShapeDtypeStruct((3 * width + 16, model), BF16),
        cost_estimate=COST(1.0),
        compiler_params=pltpu.CompilerParams(vmem_limit_bytes=VMEM_LIMIT),
        name="pack",
    )(ow, up, dn, ub)


def digit(value, b):
    return ((value >> b) & 1)[None]


def reduce_plain(keep, send, vec, dp_count):
    width, model = keep.shape[0] // 6, keep.shape[1]
    sections = 3
    keep = keep.reshape(2, 3, width, model)
    send = send[: 6 * width].reshape(2, 3, width, model)
    rows = width // dp_count
    keep = keep + swap(send, "chan", 1)
    keep = keep[0] + swap(keep[1], "chan", 2)
    if rows < 16:
        last = keep[2].reshape(width, 4, width).transpose(1, 0, 2).reshape(width, model)
        last = last.reshape(dp_count, 4, rows, width).transpose(0, 2, 1, 3)
        keep = jnp.stack([keep[0], keep[1], last.reshape(width, model)])
    keep = keep.reshape(sections, dp_count, rows, model).transpose(1, 0, 2, 3)
    vec = vec + swap(vec, "chan", 1)
    vec = sum_dp(vec + swap(vec, "chan", 2))
    return scatter_dp(keep), vec


def on_device(
    hidden_in,
    lengths_short,
    lengths_long,
    qkv_weight,
    qv_bias,
    out_weight,
    mixer_bias,
    first_gain,
    first_shift,
    up_weight,
    up_bias,
    down_weight,
    down_bias,
    second_gain,
    second_shift,
    out_grad,
):
    width, tokens = hidden_in.shape
    span = tokens // 8
    model = 4 * width
    dp_count = lax.axis_size("dp")
    chan = lax.axis_index("chan").astype(jnp.int32)
    dp = lax.axis_index("dp").astype(jnp.int32)
    me = chan[None]
    bar = lax.optimization_barrier
    fine = width // dp_count >= 16 and dp_count >= 4
    lengths = (lengths_short, lengths_long)
    w = qkv_weight[0]

    packed = pack(out_weight, up_weight, down_weight, up_bias)
    params = [mixer_bias, first_gain, first_shift, down_bias, second_gain, second_shift]
    far = swap(packed, "chan", 2)
    near = swap(packed, "chan", 1)
    x, _ = bar((hidden_in, packed))
    proj, *parts, lse = attn_fwd(me, *lengths, x, w, qv_bias)
    parts = [parts[:4], parts[4:]]
    far, near, parts = bar((far, near, parts))
    first = to_chan(parts[0])
    weights = [packed, near, far, swap(far, "chan", 1)]
    ready = prep(weights, params)
    second = to_chan(parts[1])
    blocks = dp_count if fine else 1
    hid = [hidden_in] + first[1:]
    lo, *rest = mid(0, me, first, hid, out_grad, ready, None, blocks)
    g0, carry = rest[:4], [*rest[4:], lo]
    g0, carry, second = bar((g0, carry, second))
    back0 = to_chan(g0)
    hid = [hidden_in] + second[1:]
    lo, *rest = mid(1, me, second, hid, out_grad, ready, carry, blocks)
    rest, back0 = bar((rest, back0))
    g1, (keep, send, vec) = rest[:4], rest[4:]
    recv = swap(send, "chan", 1)
    back = [*back0, *to_chan(g1)]
    parity = digit(dp, 0)

    def backward(start, count, x, carry, split):
        return attn_bwd(
            start,
            count,
            me,
            parity,
            *lengths,
            x,
            w,
            proj,
            lse,
            back,
            carry,
            dp_count,
            split,
        )

    if not fine:
        sums, vec = reduce_plain(keep, send, vec, dp_count)
        carry = backward(0, 5, hidden_in, None, 0)
        grad_input, gq, gbias = backward(5, 3, hidden_in, carry, 1)
        gq, gbias = scatter_dp(gq), sum_dp(gbias[0])
        own = width // dp_count
        mine = lax.dynamic_slice_in_dim(vec[:6], (dp * 4 + chan) * own, own, 1)
        mine = [mine[i] for i in range(6)]
        gub = lax.dynamic_slice_in_dim(vec[6:10], chan * width, width, 1).reshape(model)
        gup, gdn = sums[0], sums[1]
        gow = sums[2].reshape(-1, 4, width).transpose(1, 0, 2).reshape(model // dp_count, width).T
        gqv = jnp.concatenate([gbias[:width], gbias[2 * width :]])[None]
    else:
        rows = width // dp_count
        size = 6 * dp_count
        zero = jnp.zeros((1,), jnp.int32)
        recv = recv.reshape(size + 2, rows, model)
        keep = keep.reshape(size, rows, model)

        def stage(index, recv, chan_next, name):
            size = keep.shape[0]
            outer, inner = (1, size // 2) if chan_next else (size // 2, 1)
            return combine(index, keep, recv, vec, outer, inner, name)

        keep, send, vec = stage(parity, recv, False, "combine0")
        recv = swap(send, "dp", 1)
        x, keep = bar((hidden_in, keep))
        carry = backward(0, 5, x, None, 0)
        recv, carry = bar((recv, carry))
        keep, send, vec = stage(zero, recv, True, "combine1")
        recv = swap(send, "chan", 2)
        x, keep = bar((x, keep))
        grad_input, gk, gs, gbias = backward(5, 3, x, carry, 2)
        recv, gk, gs = bar((recv, gk, gs))
        grecv = swap(gs, "dp", 1)
        b = 1
        while b < dp_count.bit_length() - 1:
            keep, send, vec, gk = blend(
                digit(dp, b), keep, recv, vec, gk, grecv, gbias, False, f"blend{b}"
            )
            recv, grecv = swap(send, "dp", 1 << b), None
            b += 1
        index = jnp.stack(
            [
                jnp.zeros_like(dp),
                (model - (dp * 4 + chan) * rows) % model,
                (model - chan * width) % model,
            ]
        )
        gup, gdn, gow, gq, gqv, gub, *mine = blend(
            index, keep, recv, vec, gk, grecv, gbias, True, "blend"
        )
    return (
        lo,
        grad_input,
        gq.T[None],
        gqv,
        gow,
        mine[0],
        mine[1],
        mine[2],
        gup,
        gub,
        gdn,
        mine[3],
        mine[4],
        mine[5],
    )


def solution(mesh):
    in_specs = (
        P("chan", "dp"),
        P("dp"),
        P("dp"),
        P("chan", None, None),
        P("chan", None),
        P("chan", None),
        P(),
        P(),
        P(),
        P(None, "chan"),
        P("chan"),
        P(None, "chan"),
        P(),
        P(),
        P(),
        P(("dp", "chan"), None),
    )
    out_specs = (
        P(("dp", "chan"), None),
        P("chan", "dp"),
        P("chan", None, "dp"),
        P("chan", None),
        P("chan", "dp"),
        P(("dp", "chan")),
        P(("dp", "chan")),
        P(("dp", "chan")),
        P("dp", "chan"),
        P("chan"),
        P("dp", "chan"),
        P(("dp", "chan")),
        P(("dp", "chan")),
        P(("dp", "chan")),
    )
    return jax.shard_map(
        on_device, mesh=mesh, in_specs=in_specs, out_specs=out_specs, check_vma=False
    )
```

profile of v0, /device:TPU:0, one launch (start us, length us, event | category | flops | bytes accessed | tf_op | source)
XLA Modules:
  0.0 175.8 jit_solution(601956209580018048)
XLA Ops:
  0.6 2.1 %pack.1.w0 = bf16[592,768]{1,0:T(8,128)(2,1)} custom-call(bf16[192,768]{1,0:T(8,128)(2,1)} %ow.1, bf16[192,768]{1,0:T(8,128)(2,1)} %up.1, bf16[192,768]{1,0:T(8,128)(2,1)} %dn.1, f32[768]{0:T(1024)} %ub.1), custom_call_target="tpu_custom_call" | custom-call | flops 1000000000 | bytes 1000000 | tf_op jit(solution)/shard_map/pack/pallas_call | solution.py:931
  2.8 3.0 %collective-permute-start = (bf16[592,768]{1,0:T(8,128)(2,1)}, bf16[592,768]{1,0:T(8,128)(2,1)}, u32[]{:S(2)}, u32[]{:S(2)}) collective-permute-start(bf16[592,768]{1,0:T(8,128)(2,1)} %pack.1.w0), channel_id=1, source_target_pairs={{0,2},{1,3},{2,0},{3,1},{4,6},{5,7},{6,4},{7,5},{8,10},{9,11},{10,... | collective-permute-start | bytes 2727944 | tf_op jit(solution)/shard_map/ppermute | solution.py:875
  5.7 17.9 %attn_fwd.1 = (bf16[8,576,512]{2,1,0:T(8,128)(2,1)}, bf16[1,192,512]{2,1,0:T(8,128)(2,1)}, bf16[2,192,512]{2,1,0:T(8,128)(2,1)}, bf16[2,192,512]{2,1,0:T(8,128)(...) custom-call(s32[1]{0:T(128)} %bitcast.me.refs_0_, ...), custom_call_target="tpu_custom_call" | custom-call | flops 16000000000 | bytes 16000000 | tf_op jit(solution)/shard_map/attn_fwd/pallas_call | solution.py:145
  23.6 2.6 %collective-permute-done.w2 = bf16[592,768]{1,0:T(8,128)(2,1)} collective-permute-done((bf16[592,768]{1,0:T(8,128)(2,1)}, bf16[592,768]{1,0:T(8,128)(2,1)}, u32[]{:S(2)}, u32[]{:S(2)}) %collective-permute-start) | collective-permute-done | bytes 909344 | tf_op jit(solution)/shard_map/ppermute | solution.py:875
  26.7 1.7 collective-permute-start.3
  29.0 1.7 collective-permute-start.7
  30.8 9.4 %prep.1 = (bf16[768,768]{1,0:T(8,128)(2,1)}, bf16[4,768,192]{2,1,0:T(8,128)(2,1)}, bf16[4,768,192]{2,1,0:T(8,128)(2,1)}, bf16[4,192,768]{2,1,0:T(8,128)(2,1)}, b...) custom-call(bf16[592,768]{1,0:T(8,128)(2,1)} %pack.1.w0, ...), custom_call_target="tpu_custom_call" | custom-call | flops 4000000000 | bytes 4000000 | tf_op jit(solution)/shard_map/prep/pallas_call | solution.py:428
  40.2 6.5 %collective-permute-done.4.refs_3_.refs_7_ = bf16[2,192,512]{2,1,0:T(8,128)(2,1)} collective-permute-done((bf16[2,192,512]{2,1,0:T(8,128)(2,1)}, bf16[2,192,512]{2,1,0:T(8,128)(2,1)}, u32[]{:S(2)}, u32[]{:S(2)}) %collective-permute-start.4) | collective-permute-done | bytes 393248 | tf_op jit(solution)/shard_map/ppermute | solution.py:875
  46.7 23.4 %mid0.1 = (bf16[1024,768]{1,0:T(8,128)(2,1)}, bf16[2,192,512]{2,1,0:T(8,128)(2,1)}, bf16[2,192,512]{2,1,0:T(8,128)(2,1)}, bf16[2,192,512]{2,1,0:T(8,128)(2,1)}, ...) custom-call(s32[1]{0:T(128)} %bitcast.me.refs_0_, ...), custom_call_target="tpu_custom_call" | custom-call | flops 24999999488 | bytes 25000000 | tf_op jit(solution)/shard_map/mid0/pallas_call | solution.py:719
  72.4 25.7 %mid1.1 = (bf16[1024,768]{1,0:T(8,128)(2,1)}, bf16[2,192,512]{2,1,0:T(8,128)(2,1)}, bf16[2,192,512]{2,1,0:T(8,128)(2,1)}, bf16[2,192,512]{2,1,0:T(8,128)(2,1)}, ...) custom-call(s32[1]{0:T(128)} %bitcast.me.refs_0_, ...), custom_call_target="tpu_custom_call", output_to_operand_aliasing={{0}: (22, {})} | custom-call | flops 24999999488 | bytes 25000000 | tf_op jit(solution)/shard_map/mid1/pallas_call | solution.py:719
  98.7 1.6 collective-permute-start.15
  100.4 1.9 %collective-permute-done.12 = bf16[1200,768]{1,0:T(8,128)(2,1)} collective-permute-done((bf16[1200,768]{1,0:T(8,128)(2,1)}, bf16[1200,768]{1,0:T(8,128)(2,1)}, u32[]{:S(2)}, u32[]{:S(2)}) %collective-permute-start.12) | collective-permute-done | bytes 1843232 | tf_op jit(solution)/shard_map/ppermute | solution.py:875
  102.3 3.5 %combine0.1 = (bf16[24,24,768]{2,1,0:T(8,128)(2,1)}, bf16[26,24,768]{2,1,0:T(8,128)(2,1)}, f32[16,768]{1,0:T(8,128)}) custom-call(s32[1]{0:T(128)} %bitcast.2.index.refs_1_, bf16[48,24,768]{2,1,0:T(8,128)(2,1)} %bitcast.15, bf16[50,24,768]{2,1,0:T(8,128)(2,1)} %bitcast.4.recv, f32[16,768]{1,0:T(8,128)} %get-tuple-element.187.extra), custom_call_target="tpu_custom_call" | custom-call | flops 1000000000 | bytes 1000000 | tf_op jit(solution)/shard_map/combine0/pallas_call | solution.py:761
  105.8 1.7 collective-permute-start.13
  107.5 17.5 %attn_bwd0.1 = (f32[192,4096]{1,0:T(8,128)}, f32[576,192]{1,0:T(8,128)}, f32[8,576]{1,0:T(8,128)}) custom-call(s32[1]{0:T(128)} %bitcast.me.refs_0_, s32[1]{0:T(128)} %bitcast.2.index.refs_1_, s32[16]{0:T(128)} %refs_2_.5, s32[4]{0:T(128)} %refs_3_.5, bf16[192,4096]{1,0:T(8,128)(2,1)} %refs_4_.7, bf16[192,576]{1,0:T(8,128)(2,1)} %bitcast.13, ...), custom_call_target="tpu_custom_call" | custom-call | flops 20000000000 | bytes 20000000 | tf_op jit(solution)/shard_map/attn_bwd0/pallas_call | solution.py:347
  125.0 4.6 %collective-permute-done.13.recv = bf16[26,24,768]{2,1,0:T(8,128)(2,1)} collective-permute-done((bf16[26,24,768]{2,1,0:T(8,128)(2,1)}, bf16[26,24,768]{2,1,0:T(8,128)(2,1)}, u32[]{:S(2)}, u32[]{:S(2)}) %collective-permute-start.13) | collective-permute-done | bytes 958496 | tf_op jit(solution)/shard_map/ppermute | solution.py:875
  129.6 2.5 %combine1.1 = (bf16[12,24,768]{2,1,0:T(8,128)(2,1)}, bf16[14,24,768]{2,1,0:T(8,128)(2,1)}, f32[16,768]{1,0:T(8,128)}) custom-call(s32[1]{0:T(128)} %constant.28.clone.1.index, bf16[24,24,768]{2,1,0:T(8,128)(2,1)} %get-tuple-element.190.keep, bf16[26,24,768]{2,1,0:T(8,128)(2,1)} %collective-permute-done.13.recv, f32[16,768]{1,0:T(8,128)} %get-tuple-element.203.extra), custom_call_target="tpu_custom_call" | custom-call | flops 1000000000 | bytes 1000000 | tf_op jit(solution)/shard_map/combine1/pallas_call | solution.py:761
  132.2 1.7 collective-permute-start.17
  133.9 12.4 %attn_bwd5.1 = (f32[192,4096]{1,0:T(8,128)}, bf16[4,72,192]{2,1,0:T(8,128)(2,1)}, bf16[5,72,192]{2,1,0:T(8,128)(2,1)}, f32[24,192]{1,0:T(8,128)}) custom-call(s32[1]{0:T(128)} %bitcast.me.refs_0_, s32[1]{0:T(128)} %bitcast.2.index.refs_1_, s32[16]{0:T(128)} %refs_2_.5, s32[4]{0:T(128)} %refs_3_.5, ...), custom_call_target="tpu_custom_call", output_to_operand_aliasing={{0}: (13, {})} | custom-call | flops 12000000000 | bytes 12000000 | tf_op jit(solution)/shard_map/attn_bwd5/pallas_call | solution.py:347
  147.8 4.5 %collective-permute-done.18.refs_0_ = bf16[5,72,192]{2,1,0:T(8,128)(2,1)S(1)} collective-permute-done((bf16[5,72,192]{2,1,0:T(8,128)(2,1)}, bf16[5,72,192]{2,1,0:T(8,128)(2,1)S(1)}, u32[]{:S(2)}, u32[]{:S(2)}) %collective-permute-start.18) | collective-permute-done | bytes 138272 | tf_op jit(solution)/shard_map/ppermute | solution.py:875
  157.0 1.6 collective-permute-start.19
  158.6 6.5 %collective-permute-done.19.wr = bf16[9,24,768]{2,1,0:T(8,128)(2,1)S(1)} collective-permute-done((bf16[9,24,768]{2,1,0:T(8,128)(2,1)S(1)}, bf16[9,24,768]{2,1,0:T(8,128)(2,1)S(1)}, u32[]{:S(2)}, u32[]{:S(2)}) %collective-permute-start.19) | collective-permute-done | bytes 331808 | tf_op jit(solution)/shard_map/ppermute | solution.py:875
  165.2 2.7 %collective-permute-start.20 = (bf16[5,24,768]{2,1,0:T(8,128)(2,1)S(1)}, bf16[5,24,768]{2,1,0:T(8,128)(2,1)S(1)}, u32[]{:S(2)}, u32[]{:S(2)}) collective-permute-start(bf16[5,24,768]{2,1,0:T(8,128)(2,1)S(1)} %get-tuple-element.227), channel_id=1, source_target_pairs={{0,16},{4,20},{8,24},{12,28},{16,0},{20,4},{24,8},{28,12},{1,17},{... | collective-permute-start | bytes 552968 | tf_op jit(solution)/shard_map/ppermute | solution.py:875
  168.0 6.2 %collective-permute-done.20.wr = bf16[5,24,768]{2,1,0:T(8,128)(2,1)S(1)} collective-permute-done((bf16[5,24,768]{2,1,0:T(8,128)(2,1)S(1)}, bf16[5,24,768]{2,1,0:T(8,128)(2,1)S(1)}, u32[]{:S(2)}, u32[]{:S(2)}) %collective-permute-start.20) | collective-permute-done | bytes 184352 | tf_op jit(solution)/shard_map/ppermute | solution.py:875
  (39 shorter events, 11.9 us)
Async XLA Ops:
  2.8 23.5 %collective-permute-start = (bf16[592,768]{1,0:T(8,128)(2,1)}, bf16[592,768]{1,0:T(8,128)(2,1)}, u32[]{:S(2)}, u32[]{:S(2)}) collective-permute-start(bf16[592,768]{1,0:T(8,128)(2,1)} %pack.1.w0), channel_id=1, source_target_pairs={{0,2},{1,3},{2,0},{3,1},{4,6},{5,7},{6,4},{7,5},{8,10},{9,11},{10,... | collective-permute-start | bytes 2727944 | tf_op jit(solution)/shard_map/ppermute | solution.py:875
  5.7 20.5 %collective-permute-start.1 = (bf16[592,768]{1,0:T(8,128)(2,1)}, bf16[592,768]{1,0:T(8,128)(2,1)}, u32[]{:S(2)}, u32[]{:S(2)}) collective-permute-start(bf16[592,768]{1,0:T(8,128)(2,1)} %pack.1.w0), channel_id=1, source_target_pairs={{0,1},{1,0},{2,3},{3,2},{4,5},{5,4},{6,7},{7,6},{8,9},{9,8},{10,11... | collective-permute-start | bytes 2727944 | tf_op jit(solution)/shard_map/ppermute | solution.py:875
  26.2 2.8 %collective-permute-start.5 = (bf16[592,768]{1,0:T(8,128)(2,1)}, bf16[592,768]{1,0:T(8,128)(2,1)}, u32[]{:S(2)}, u32[]{:S(2)}) collective-permute-start(bf16[592,768]{1,0:T(8,128)(2,1)} %collective-permute-done.w2), channel_id=1, source_target_pairs={{0,1},{1,0},{2,3},{3,2},{4,5},{5,4},{6,7},{7,6},{8,9},{9,8},{10,11... | collective-permute-start | bytes 2727944 | tf_op jit(solution)/shard_map/ppermute | solution.py:875
  26.2 13.9 %collective-permute-start.2 = (bf16[2,192,512]{2,1,0:T(8,128)(2,1)}, bf16[2,192,512]{2,1,0:T(8,128)(2,1)}, u32[]{:S(2)}, u32[]{:S(2)}) collective-permute-start(bf16[2,192,512]{2,1,0:T(8,128)(2,1)} %get-tuple-element.138), channel_id=1, source_target_pairs={{0,1},{1,0},{2,3},{3,2},{4,5},{5,4},{6,7},{7,6},{8,9},{9,8},{10,11... | collective-permute-start | bytes 1179656 | tf_op jit(solution)/shard_map/ppermute | solution.py:875
  26.7 13.5 %collective-permute-start.3 = (bf16[2,192,512]{2,1,0:T(8,128)(2,1)}, bf16[2,192,512]{2,1,0:T(8,128)(2,1)}, u32[]{:S(2)}, u32[]{:S(2)}) collective-permute-start(bf16[2,192,512]{2,1,0:T(8,128)(2,1)} %get-tuple-element.139), channel_id=1, source_target_pairs={{0,2},{1,3},{2,0},{3,1},{4,6},{5,7},{6,4},{7,5},{8,10},{9,11},{10,... | collective-permute-start | bytes 1179656 | tf_op jit(solution)/shard_map/ppermute | solution.py:875
  28.5 18.2 %collective-permute-start.4 = (bf16[2,192,512]{2,1,0:T(8,128)(2,1)}, bf16[2,192,512]{2,1,0:T(8,128)(2,1)}, u32[]{:S(2)}, u32[]{:S(2)}) collective-permute-start(bf16[2,192,512]{2,1,0:T(8,128)(2,1)} %get-tuple-element.140), channel_id=1, source_target_pairs={{0,3},{1,2},{2,1},{3,0},{4,7},{5,6},{6,5},{7,4},{8,11},{9,10},{10,... | collective-permute-start | bytes 1179656 | tf_op jit(solution)/shard_map/ppermute | solution.py:875
  28.5 41.6 %collective-permute-start.6 = (bf16[2,192,512]{2,1,0:T(8,128)(2,1)}, bf16[2,192,512]{2,1,0:T(8,128)(2,1)}, u32[]{:S(2)}, u32[]{:S(2)}) collective-permute-start(bf16[2,192,512]{2,1,0:T(8,128)(2,1)} %get-tuple-element.161), channel_id=1, source_target_pairs={{0,1},{1,0},{2,3},{3,2},{4,5},{5,4},{6,7},{7,6},{8,9},{9,8},{10,11... | collective-permute-start | bytes 1179656 | tf_op jit(solution)/shard_map/ppermute | solution.py:875
  29.0 41.1 %collective-permute-start.7 = (bf16[2,192,512]{2,1,0:T(8,128)(2,1)}, bf16[2,192,512]{2,1,0:T(8,128)(2,1)}, u32[]{:S(2)}, u32[]{:S(2)}) collective-permute-start(bf16[2,192,512]{2,1,0:T(8,128)(2,1)} %get-tuple-element.162), channel_id=1, source_target_pairs={{0,2},{1,3},{2,0},{3,1},{4,6},{5,7},{6,4},{7,5},{8,10},{9,11},{10,... | collective-permute-start | bytes 1179656 | tf_op jit(solution)/shard_map/ppermute | solution.py:875
  40.2 30.0 %collective-permute-start.8 = (bf16[2,192,512]{2,1,0:T(8,128)(2,1)}, bf16[2,192,512]{2,1,0:T(8,128)(2,1)}, u32[]{:S(2)}, u32[]{:S(2)}) collective-permute-start(bf16[2,192,512]{2,1,0:T(8,128)(2,1)} %get-tuple-element.163), channel_id=1, source_target_pairs={{0,3},{1,2},{2,1},{3,0},{4,7},{5,6},{6,5},{7,4},{8,11},{9,10},{10,... | collective-permute-start | bytes 1179656 | tf_op jit(solution)/shard_map/ppermute | solution.py:875
  70.2 27.9 %collective-permute-start.10 = (bf16[2,192,512]{2,1,0:T(8,128)(2,1)}, bf16[2,192,512]{2,1,0:T(8,128)(2,1)}, u32[]{:S(2)}, u32[]{:S(2)}) collective-permute-start(bf16[2,192,512]{2,1,0:T(8,128)(2,1)} %get-tuple-element.183), channel_id=1, source_target_pairs={{0,2},{1,3},{2,0},{3,1},{4,6},{5,7},{6,4},{7,5},{8,10},{9,11},{10,... | collective-permute-start | bytes 1179656 | tf_op jit(solution)/shard_map/ppermute | solution.py:875
  70.8 27.3 %collective-permute-start.11 = (bf16[2,192,512]{2,1,0:T(8,128)(2,1)}, bf16[2,192,512]{2,1,0:T(8,128)(2,1)}, u32[]{:S(2)}, u32[]{:S(2)}) collective-permute-start(bf16[2,192,512]{2,1,0:T(8,128)(2,1)} %get-tuple-element.184), channel_id=1, source_target_pairs={{0,3},{1,2},{2,1},{3,0},{4,7},{5,6},{6,5},{7,4},{8,11},{9,10},{10,... | collective-permute-start | bytes 1179656 | tf_op jit(solution)/shard_map/ppermute | solution.py:875
  72.2 25.9 %collective-permute-start.9 = (bf16[2,192,512]{2,1,0:T(8,128)(2,1)}, bf16[2,192,512]{2,1,0:T(8,128)(2,1)}, u32[]{:S(2)}, u32[]{:S(2)}) collective-permute-start(bf16[2,192,512]{2,1,0:T(8,128)(2,1)} %get-tuple-element.182), channel_id=1, source_target_pairs={{0,1},{1,0},{2,3},{3,2},{4,5},{5,4},{6,7},{7,6},{8,9},{9,8},{10,11... | collective-permute-start | bytes 1179656 | tf_op jit(solution)/shard_map/ppermute | solution.py:875
  98.1 4.2 %collective-permute-start.12 = (bf16[1200,768]{1,0:T(8,128)(2,1)}, bf16[1200,768]{1,0:T(8,128)(2,1)}, u32[]{:S(2)}, u32[]{:S(2)}) collective-permute-start(bf16[1200,768]{1,0:T(8,128)(2,1)} %get-tuple-element.186), channel_id=1, source_target_pairs={{0,1},{1,0},{2,3},{3,2},{4,5},{5,4},{6,7},{7,6},{8,9},{9,8},{10,11... | collective-permute-start | bytes 5529608 | tf_op jit(solution)/shard_map/ppermute | solution.py:875
  98.5 35.3 %collective-permute-start.14 = (bf16[2,192,512]{2,1,0:T(8,128)(2,1)}, bf16[2,192,512]{2,1,0:T(8,128)(2,1)}, u32[]{:S(2)}, u32[]{:S(2)}) collective-permute-start(bf16[2,192,512]{2,1,0:T(8,128)(2,1)} %get-tuple-element.206), channel_id=1, source_target_pairs={{0,1},{1,0},{2,3},{3,2},{4,5},{5,4},{6,7},{7,6},{8,9},{9,8},{10,11... | collective-permute-start | bytes 1179656 | tf_op jit(solution)/shard_map/ppermute | solution.py:875
  98.7 35.2 %collective-permute-start.15 = (bf16[2,192,512]{2,1,0:T(8,128)(2,1)}, bf16[2,192,512]{2,1,0:T(8,128)(2,1)}, u32[]{:S(2)}, u32[]{:S(2)}) collective-permute-start(bf16[2,192,512]{2,1,0:T(8,128)(2,1)} %get-tuple-element.207), channel_id=1, source_target_pairs={{0,2},{1,3},{2,0},{3,1},{4,6},{5,7},{6,4},{7,5},{8,10},{9,11},{10,... | collective-permute-start | bytes 1179656 | tf_op jit(solution)/shard_map/ppermute | solution.py:875
  100.3 33.6 %collective-permute-start.16 = (bf16[2,192,512]{2,1,0:T(8,128)(2,1)}, bf16[2,192,512]{2,1,0:T(8,128)(2,1)}, u32[]{:S(2)}, u32[]{:S(2)}) collective-permute-start(bf16[2,192,512]{2,1,0:T(8,128)(2,1)} %get-tuple-element.208), channel_id=1, source_target_pairs={{0,3},{1,2},{2,1},{3,0},{4,7},{5,6},{6,5},{7,4},{8,11},{9,10},{10,... | collective-permute-start | bytes 1179656 | tf_op jit(solution)/shard_map/ppermute | solution.py:875
  105.8 23.8 %collective-permute-start.13 = (bf16[26,24,768]{2,1,0:T(8,128)(2,1)}, bf16[26,24,768]{2,1,0:T(8,128)(2,1)}, u32[]{:S(2)}, u32[]{:S(2)}) collective-permute-start(bf16[26,24,768]{2,1,0:T(8,128)(2,1)} %get-tuple-element.191), channel_id=1, source_target_pairs={{0,4},{4,0},{8,12},{12,8},{16,20},{20,16},{24,28},{28,24},{1,5},{5... | collective-permute-start | bytes 2875400 | tf_op jit(solution)/shard_map/ppermute | solution.py:875
  132.2 14.1 %collective-permute-start.17 = (bf16[14,24,768]{2,1,0:T(8,128)(2,1)}, bf16[14,24,768]{2,1,0:T(8,128)(2,1)}, u32[]{:S(2)}, u32[]{:S(2)}) collective-permute-start(bf16[14,24,768]{2,1,0:T(8,128)(2,1)} %get-tuple-element.214), channel_id=1, source_target_pairs={{0,2},{1,3},{2,0},{3,1},{4,6},{5,7},{6,4},{7,5},{8,10},{9,11},{10,... | collective-permute-start | bytes 1548296 | tf_op jit(solution)/shard_map/ppermute | solution.py:875
  146.3 6.0 %collective-permute-start.18 = (bf16[5,72,192]{2,1,0:T(8,128)(2,1)}, bf16[5,72,192]{2,1,0:T(8,128)(2,1)S(1)}, u32[]{:S(2)}, u32[]{:S(2)}) collective-permute-start(bf16[5,72,192]{2,1,0:T(8,128)(2,1)} %get-tuple-element.220), channel_id=1, source_target_pairs={{0,4},{4,0},{8,12},{12,8},{16,20},{20,16},{24,28},{28,24},{1,5},{5... | collective-permute-start | bytes 414728 | tf_op jit(solution)/shard_map/ppermute | solution.py:875
  152.3 1.0 copy-start
  153.3 0.9 copy-start.1
  154.2 0.8 copy-start.2
  157.0 8.1 %collective-permute-start.19 = (bf16[9,24,768]{2,1,0:T(8,128)(2,1)S(1)}, bf16[9,24,768]{2,1,0:T(8,128)(2,1)S(1)}, u32[]{:S(2)}, u32[]{:S(2)}) collective-permute-start(bf16[9,24,768]{2,1,0:T(8,128)(2,1)S(1)} %get-tuple-element.223), channel_id=1, source_target_pairs={{0,8},{4,12},{8,0},{12,4},{16,24},{20,28},{24,16},{28,20},{1,9},{5... | collective-permute-start | bytes 995336 | tf_op jit(solution)/shard_map/ppermute | solution.py:875
  165.2 9.0 %collective-permute-start.20 = (bf16[5,24,768]{2,1,0:T(8,128)(2,1)S(1)}, bf16[5,24,768]{2,1,0:T(8,128)(2,1)S(1)}, u32[]{:S(2)}, u32[]{:S(2)}) collective-permute-start(bf16[5,24,768]{2,1,0:T(8,128)(2,1)S(1)} %get-tuple-element.227), channel_id=1, source_target_pairs={{0,16},{4,20},{8,24},{12,28},{16,0},{20,4},{24,8},{28,12},{1,17},{... | collective-permute-start | bytes 552968 | tf_op jit(solution)/shard_map/ppermute | solution.py:875
  (1 other events, 0.7 us)
where the time goes:
time: 176 us
  Pallas kernels  117 us (66%)
  waiting for transfers between devices  33 us (19%)
  starting transfers between devices  21.2 us (12%)
  local copies, waits for them, and re-layouts  3.46 us (2%)
    pallas_call x2, Pallas kernels, mid(): pl.pallas_call(functools.partial(mid_kernel, half, width, blocks), grid_s...  49.1 us
    ppermute x21, waiting for transfers between devices, swap(): return lax.ppermute(value, axis, [(i, i ^ bit) for i in range(count)])  33 us
    pallas_call x2, Pallas kernels, attn_bwd(): pl.pallas_call(functools.partial(attn_bwd_kernel, first, count, heads, sh...  29.9 us
    ppermute x21, starting transfers between devices, swap(): return lax.ppermute(value, axis, [(i, i ^ bit) for i in range(count)])  21.2 us
    pallas_call x1, Pallas kernels, attn_fwd(): pl.pallas_call(functools.partial(attn_fwd_kernel, heads, short_blocks), g...  17.9 us
    pallas_call x1, Pallas kernels, prep(): pl.pallas_call(prep_kernel, in_specs=[vmem] * 10, out_specs=[vmem] * len(...  9.37 us
    pallas_call x2, Pallas kernels, combine(): pl.pallas_call(functools.partial(combine_kernel, size, outer, inner), in_...  6.04 us
  transfers between devices with their start and end apart: 21, of which 8 were waited for; matrix products, arithmetic and copies ran while one was open for 0% of the time, Pallas kernels for 64%

commit v1 on v0

--- a/solution.py
+++ b/solution.py
@@ -95,36 +95,38 @@
 
     proj[0] = (dot(w[...], x[...], 0, 0) + bcol[:, 0:1]).astype(BF16)
 
-    def run(seq_len, lens, first):
+    def run(seq_len, lens, first, together):
         score_operands(
             heads, span, seq_len, lens, first, proj[0, :width], proj[0, width : 2 * width], qa, ka
         )
         items = [(i, h) for i in range(span // seq_len) for h in range(heads)]
+        groups = [items[n : n + together] for n in range(0, len(items), together)]
 
         def score(i, h):
             cols = slice(i * seq_len, (i + 1) * seq_len)
             return dot(ka[h, :, cols], qa[h, :, cols], 0, 0)
 
-        s = score(*items[0])
-        for n, (i, h) in enumerate(items):
-            later = score(*items[n + 1]) if n + 1 < len(items) else None
-            cols = slice(i * seq_len, (i + 1) * seq_len)
-            m = jnp.max(s, axis=0, keepdims=True)
-            e = jnp.exp2(s - m)
-            total = jnp.sum(e, axis=0, keepdims=True)
-            val = proj[0, 2 * width + h * HD : 2 * width + (h + 1) * HD, cols]
-            c = dot(val, e.astype(BF16), 1, 0) * (1.0 / total)
-            scr[h * HD : (h + 1) * HD, cols] = c.astype(BF16)
-            lse[0, h : h + 1, cols] = m + jnp.log2(total)
-            s = later
+        scores = [score(*item) for item in groups[0]]
+        for n, group in enumerate(groups):
+            later = [score(*item) for item in groups[n + 1]] if n + 1 < len(groups) else None
+            tops = [jnp.max(s, axis=0, keepdims=True) for s in scores]
+            exps = [jnp.exp2(s - m) for s, m in zip(scores, tops)]
+            sums = [jnp.sum(e, axis=0, keepdims=True) for e in exps]
+            for (i, h), m, e, total in zip(group, tops, exps, sums):
+                cols = slice(i * seq_len, (i + 1) * seq_len)
+                val = proj[0, 2 * width + h * HD : 2 * width + (h + 1) * HD, cols]
+                c = dot(val, e.astype(BF16), 1, 0) * (1.0 / total)
+                scr[h * HD : (h + 1) * HD, cols] = c.astype(BF16)
+                lse[0, h : h + 1, cols] = m + jnp.log2(total)
+            scores = later
 
     @pl.when(block < short_blocks)
     def _():
-        run(LS, lens_s, block * (span // LS))
+        run(LS, lens_s, block * (span // LS), 6)
 
     @pl.when(block >= short_blocks)
     def _():
-        run(LL, lens_l, (block - short_blocks) * (span // LL))
+        run(LL, lens_l, (block - short_blocks) * (span // LL), 1)
 
     for i, out in enumerate(outs):
 
@@ -211,11 +213,12 @@
         def _():
             gsc[...] = g[...]
 
-    def run(seq_len, lens, first):
+    def run(seq_len, lens, first, together):
         score_operands(
             heads, span, seq_len, lens, first, proj[0, :width], proj[0, width : 2 * width], qa, ka
         )
         items = [(i, h) for i in range(span // seq_len) for h in range(heads)]
+        groups = [items[n : n + together] for n in range(0, len(items), together)]
 
         def score(i, h):
             cols = slice(i * seq_len, (i + 1) * seq_len)
@@ -223,30 +226,31 @@
             go = gsc[0, h * HD : (h + 1) * HD, cols]
             return dot(ka[h, :, cols], qa[h, :, cols], 0, 0), dot(val, go, 0, 0)
 
-        pair = score(*items[0])
-        for n, (i, h) in enumerate(items):
-            later = score(*items[n + 1]) if n + 1 < len(items) else None
-            cols = slice(i * seq_len, (i + 1) * seq_len)
-            rq, rk, rv = [slice(j * width + h * HD, j * width + (h + 1) * HD) for j in range(3)]
-            q = proj[0, rq, cols]
-            key = proj[0, rk, cols]
-            go = gsc[0, h * HD : (h + 1) * HD, cols]
-            s, gp = pair
-            p = jnp.exp2(s - lse[0, h : h + 1, cols])
-            inner = jnp.sum(p * gp, axis=0, keepdims=True)
-            g = (p * (gp - inner)).astype(BF16)
-            dproj[rq, cols] = (dot(key, g, 1, 0) * scale).astype(BF16)
-            dproj[rk, cols] = (dot(q, g, 1, 1) * scale).astype(BF16)
-            dproj[rv, cols] = dot(go, p.astype(BF16), 1, 1).astype(BF16)
-            pair = later
+        pairs = [score(*item) for item in groups[0]]
+        for n, group in enumerate(groups):
+            later = [score(*item) for item in groups[n + 1]] if n + 1 < len(groups) else None
+            ps = []
+            for (i, h), (s, _) in zip(group, pairs):
+                cols = slice(i * seq_len, (i + 1) * seq_len)
+                ps.append(jnp.exp2(s - lse[0, h : h + 1, cols]))
+            inner = [jnp.sum(p * gp, axis=0, keepdims=True) for p, (_, gp) in zip(ps, pairs)]
+            gs = [(p * (gp - r)).astype(BF16) for p, (_, gp), r in zip(ps, pairs, inner)]
+            for (i, h), p, g in zip(group, ps, gs):
+                cols = slice(i * seq_len, (i + 1) * seq_len)
+                rq, rk, rv = [slice(j * width + h * HD, j * width + (h + 1) * HD) for j in range(3)]
+                go = gsc[0, h * HD : (h + 1) * HD, cols]
+                dproj[rq, cols] = (dot(proj[0, rk, cols], g, 1, 0) * scale).astype(BF16)
+                dproj[rk, cols] = (dot(proj[0, rq, cols], g, 1, 1) * scale).astype(BF16)
+                dproj[rv, cols] = dot(go, p.astype(BF16), 1, 1).astype(BF16)
+            pairs = later
 
     @pl.when(block < short_blocks)
     def _():
-        run(LS, lens_s, block * (span // LS))
+        run(LS, lens_s, block * (span // LS), 4)
 
     @pl.when(block >= short_blocks)
     def _():
-        run(LL, lens_l, (block - short_blocks) * (span // LL))
+        run(LL, lens_l, (block - short_blocks) * (span // LL), 1)
 
     gin[...] = dot(w[...], dproj[...], 1, 0) + gsc[1].astype(F32)
     part = dot(dproj[...], x[...], 1, 1)
@@ -769,6 +773,68 @@
     )(index, keep, recv, extra)
 
 
+def pulled(kernel, count, index, *refs):
+    bufs, sem = refs[-count - 1 : -1], refs[-1]
+    copies = [pltpu.make_async_copy(refs[i], bufs[i], sem.at[i]) for i in range(count)]
+    for c in copies:
+        c.start()
+    for c in copies:
+        c.wait()
+    kernel(index, *bufs, *refs[count : -count - 1])
+
+
+def pull_call(kernel, count, index, args, shapes, name):
+    vmem = pl.BlockSpec(memory_space=pltpu.VMEM)
+    return pl.pallas_call(
+        functools.partial(pulled, kernel, count),
+        in_specs=[pl.BlockSpec(memory_space=pltpu.SMEM)]
+        + [pl.BlockSpec(memory_space=pltpu.HBM)] * count
+        + [vmem] * (len(args) - count),
+        out_specs=[vmem] * len(shapes),
+        out_shape=shapes,
+        scratch_shapes=[pltpu.VMEM(a.shape, a.dtype) for a in args[:count]]
+        + [pltpu.SemaphoreType.DMA((count,))],
+        cost_estimate=COST(1.0),
+        compiler_params=pltpu.CompilerParams(vmem_limit_bytes=VMEM_SMALL),
+        name=name,
+    )(index, *args)
+
+
+def combine_early(index, keep, recv, extra, name):
+    size, rows, lanes = keep.shape
+    shapes = [
+        jax.ShapeDtypeStruct((size // 2, rows, lanes), BF16),
+        jax.ShapeDtypeStruct((size // 2 + 2, rows, lanes), BF16),
+        jax.ShapeDtypeStruct(extra.shape, F32),
+    ]
+    kernel = functools.partial(combine_kernel, size, size // 2, 1)
+    return pull_call(kernel, 3, index, [keep, recv, extra], shapes, name)
+
+
+def qkv_kernel(index, qk, qb, qr, kept, sent, qb_out):
+    size = qk.shape[0]
+    more = qb[...] + (qr[size, :24].astype(F32) + qr[size, 24:48].astype(F32))
+    qb_out[...] = more
+    hi = more.astype(BF16)
+    sent[size // 2, :24] = hi
+    sent[size // 2, 24:48] = (more - hi.astype(F32)).astype(BF16)
+    mine = index[0]
+    for i in range(size // 2):
+        a, b = 2 * i + mine, 2 * i + 1 - mine
+        kept[i] = (qk[a].astype(F32) + qr[a].astype(F32)).astype(BF16)
+        sent[i] = (qk[b].astype(F32) + qr[b].astype(F32)).astype(BF16)
+
+
+def qkv_stage(index, qk, qb, qr, name):
+    size, rows, lanes = qk.shape
+    shapes = [
+        jax.ShapeDtypeStruct((size // 2, rows, lanes), BF16),
+        jax.ShapeDtypeStruct((size // 2 + 1, rows, lanes), BF16),
+        jax.ShapeDtypeStruct(qb.shape, F32),
+    ]
+    return pull_call(qkv_kernel, 2, index, [qk, qb, qr], shapes, name)
+
+
 def blend_kernel(joint, last, index, wk, wr, vec, qk, *refs):
     if not joint:
         qr, qb, refs = refs[0], refs[1], refs[2:]
@@ -987,7 +1053,7 @@
     dp = lax.axis_index("dp").astype(jnp.int32)
     me = chan[None]
     bar = lax.optimization_barrier
-    fine = width // dp_count >= 16 and dp_count >= 4
+    fine = width // dp_count >= 16 and dp_count >= 8
     lengths = (lengths_short, lengths_long)
     w = qkv_weight[0]
 
@@ -1069,7 +1135,14 @@
         grad_input, gk, gs, gbias = backward(5, 3, x, carry, 2)
         recv, gk, gs = bar((recv, gk, gs))
         grecv = swap(gs, "dp", 1)
-        b = 1
+        second = digit(dp, 1)
+        keep, send, vec = combine_early(second, keep, recv, vec, "combine2")
+        recv = swap(send, "dp", 2)
+        grecv, keep = bar((grecv, keep))
+        gk, gs, gbias = qkv_stage(second, gk, gbias, grecv, "qkv2")
+        grecv = swap(gs, "dp", 2)
+        recv, gk = bar((recv, gk))
+        b = 2
         while b < dp_count.bit_length() - 1:
             keep, send, vec, gk = blend(
                 digit(dp, b), keep, recv, vec, gk, grecv, gbias, False, f"blend{b}"

time: 176 us -> 172 us (0.977)
  Pallas kernels: 117 us -> 113 us
    pallas_call x1, Pallas kernels: 17.9 us -> 15.3 us  [attn_fwd(): pl.pallas_call(functools.partial(attn_fwd_kernel, heads, short_blocks), g...]
    pallas_call x2, Pallas kernels: 29.9 us -> 27.6 us  [attn_bwd(): pl.pallas_call(functools.partial(attn_bwd_kernel, first, count, heads, sh...]
    ppermute x21 -> x22, starting transfers between devices: 21.2 us -> 22.4 us  [swap(): return lax.ppermute(value, axis, [(i, i ^ bit) for i in range(count)])]
    ppermute x21 -> x22, waiting for transfers between devices: 33 us -> 34 us  [swap(): return lax.ppermute(value, axis, [(i, i ^ bit) for i in range(count)])]
  transfers between devices with their start and end apart: 21 -> 22, of which waited for: 8 -> 8; matrix products, arithmetic and copies ran while one was open for 0% -> 0% of each run, Pallas kernels for 64% -> 63%
where the time goes in v1:
time: 172 us
  Pallas kernels  113 us (66%)
  waiting for transfers between devices  34 us (20%)
  starting transfers between devices  22.4 us (13%)
  local copies, waits for them, and re-layouts  1.82 us (1%)
    pallas_call x2, Pallas kernels, mid(): pl.pallas_call(functools.partial(mid_kernel, half, width, blocks), grid_s...  49.1 us
    ppermute x22, waiting for transfers between devices, swap(): return lax.ppermute(value, axis, [(i, i ^ bit) for i in range(count)])  34 us
    pallas_call x2, Pallas kernels, attn_bwd(): pl.pallas_call(functools.partial(attn_bwd_kernel, first, count, heads, sh...  27.6 us
    ppermute x22, starting transfers between devices, swap(): return lax.ppermute(value, axis, [(i, i ^ bit) for i in range(count)])  22.4 us
    pallas_call x1, Pallas kernels, attn_fwd(): pl.pallas_call(functools.partial(attn_fwd_kernel, heads, short_blocks), g...  15.3 us
    pallas_call x1, Pallas kernels, prep(): pl.pallas_call(prep_kernel, in_specs=[vmem] * 10, out_specs=[vmem] * len(...  9.38 us
    pallas_call x2, Pallas kernels, combine(): pl.pallas_call(functools.partial(combine_kernel, size, outer, inner), in_...  6.04 us
  transfers between devices with their start and end apart: 22, of which 8 were waited for; matrix products, arithmetic and copies ran while one was open for 0% of the time, Pallas kernels for 63%

profile of v1, /device:TPU:0, one launch (start us, length us, event | category | flops | bytes accessed | tf_op | source)
XLA Modules:
  0.0 172.0 jit_solution(7642524998978375593)
XLA Ops:
  0.6 2.1 %pack.1.w0 = bf16[592,768]{1,0:T(8,128)(2,1)} custom-call(bf16[192,768]{1,0:T(8,128)(2,1)} %ow.1, bf16[192,768]{1,0:T(8,128)(2,1)} %up.1, bf16[192,768]{1,0:T(8,128)(2,1)} %dn.1, f32[768]{0:T(1024)} %ub.1), custom_call_target="tpu_custom_call" | custom-call | flops 1000000000 | bytes 1000000 | tf_op jit(solution)/shard_map/pack/pallas_call | solution.py:997
  2.8 3.0 %collective-permute-start = (bf16[592,768]{1,0:T(8,128)(2,1)}, bf16[592,768]{1,0:T(8,128)(2,1)}, u32[]{:S(2)}, u32[]{:S(2)}) collective-permute-start(bf16[592,768]{1,0:T(8,128)(2,1)} %pack.1.w0), channel_id=1, source_target_pairs={{0,2},{1,3},{2,0},{3,1},{4,6},{5,7},{6,4},{7,5},{8,10},{9,11},{10,... | collective-permute-start | bytes 2727944 | tf_op jit(solution)/shard_map/ppermute | solution.py:941
  5.7 15.3 %attn_fwd.1 = (bf16[8,576,512]{2,1,0:T(8,128)(2,1)}, bf16[1,192,512]{2,1,0:T(8,128)(2,1)}, bf16[2,192,512]{2,1,0:T(8,128)(2,1)}, bf16[2,192,512]{2,1,0:T(8,128)(...) custom-call(s32[1]{0:T(128)} %bitcast.me.refs_0_, ...), custom_call_target="tpu_custom_call" | custom-call | flops 16000000000 | bytes 16000000 | tf_op jit(solution)/shard_map/attn_fwd/pallas_call | solution.py:147
  21.0 5.2 %collective-permute-done.w2 = bf16[592,768]{1,0:T(8,128)(2,1)} collective-permute-done((bf16[592,768]{1,0:T(8,128)(2,1)}, bf16[592,768]{1,0:T(8,128)(2,1)}, u32[]{:S(2)}, u32[]{:S(2)}) %collective-permute-start) | collective-permute-done | bytes 909344 | tf_op jit(solution)/shard_map/ppermute | solution.py:941
  26.7 1.7 %collective-permute-start.3 = (bf16[2,192,512]{2,1,0:T(8,128)(2,1)}, bf16[2,192,512]{2,1,0:T(8,128)(2,1)}, u32[]{:S(2)}, u32[]{:S(2)}) collective-permute-start(bf16[2,192,512]{2,1,0:T(8,128)(2,1)} %get-tuple-element.145), channel_id=1, source_target_pairs={{0,2},{1,3},{2,0},{3,1},{4,6},{5,7},{6,4},{7,5},{8,10},{9,11},{10,... | collective-permute-start | bytes 1179656 | tf_op jit(solution)/shard_map/ppermute | solution.py:941
  29.0 1.7 %collective-permute-start.7 = (bf16[2,192,512]{2,1,0:T(8,128)(2,1)}, bf16[2,192,512]{2,1,0:T(8,128)(2,1)}, u32[]{:S(2)}, u32[]{:S(2)}) collective-permute-start(bf16[2,192,512]{2,1,0:T(8,128)(2,1)} %get-tuple-element.168), channel_id=1, source_target_pairs={{0,2},{1,3},{2,0},{3,1},{4,6},{5,7},{6,4},{7,5},{8,10},{9,11},{10,... | collective-permute-start | bytes 1179656 | tf_op jit(solution)/shard_map/ppermute | solution.py:941
  30.8 9.4 %prep.1 = (bf16[768,768]{1,0:T(8,128)(2,1)}, bf16[4,768,192]{2,1,0:T(8,128)(2,1)}, bf16[4,768,192]{2,1,0:T(8,128)(2,1)}, bf16[4,192,768]{2,1,0:T(8,128)(2,1)}, b...) custom-call(bf16[592,768]{1,0:T(8,128)(2,1)} %pack.1.w0, ...), custom_call_target="tpu_custom_call" | custom-call | flops 4000000000 | bytes 4000000 | tf_op jit(solution)/shard_map/prep/pallas_call | solution.py:432
  40.3 6.5 %collective-permute-done.4.refs_3_.refs_7_ = bf16[2,192,512]{2,1,0:T(8,128)(2,1)} collective-permute-done((bf16[2,192,512]{2,1,0:T(8,128)(2,1)}, bf16[2,192,512]{2,1,0:T(8,128)(2,1)}, u32[]{:S(2)}, u32[]{:S(2)}) %collective-permute-start.4) | collective-permute-done | bytes 393248 | tf_op jit(solution)/shard_map/ppermute | solution.py:941
  46.7 23.4 %mid0.1 = (bf16[1024,768]{1,0:T(8,128)(2,1)}, bf16[2,192,512]{2,1,0:T(8,128)(2,1)}, bf16[2,192,512]{2,1,0:T(8,128)(2,1)}, bf16[2,192,512]{2,1,0:T(8,128)(2,1)}, ...) custom-call(s32[1]{0:T(128)} %bitcast.me.refs_0_, ...), custom_call_target="tpu_custom_call" | custom-call | flops 24999999488 | bytes 25000000 | tf_op jit(solution)/shard_map/mid0/pallas_call | solution.py:723
  72.4 25.7 %mid1.1 = (bf16[1024,768]{1,0:T(8,128)(2,1)}, bf16[2,192,512]{2,1,0:T(8,128)(2,1)}, bf16[2,192,512]{2,1,0:T(8,128)(2,1)}, bf16[2,192,512]{2,1,0:T(8,128)(2,1)}, ...) custom-call(s32[1]{0:T(128)} %bitcast.me.refs_0_, ...), custom_call_target="tpu_custom_call", output_to_operand_aliasing={{0}: (22, {})} | custom-call | flops 24999999488 | bytes 25000000 | tf_op jit(solution)/shard_map/mid1/pallas_call | solution.py:723
  98.7 1.6 collective-permute-start.15
  100.4 1.9 %collective-permute-done.12 = bf16[1200,768]{1,0:T(8,128)(2,1)} collective-permute-done((bf16[1200,768]{1,0:T(8,128)(2,1)}, bf16[1200,768]{1,0:T(8,128)(2,1)}, u32[]{:S(2)}, u32[]{:S(2)}) %collective-permute-start.12) | collective-permute-done | bytes 1843232 | tf_op jit(solution)/shard_map/ppermute | solution.py:941
  102.3 3.5 %combine0.1 = (bf16[24,24,768]{2,1,0:T(8,128)(2,1)}, bf16[26,24,768]{2,1,0:T(8,128)(2,1)}, f32[16,768]{1,0:T(8,128)}) custom-call(s32[1]{0:T(128)} %bitcast.2.index.refs_1_, bf16[48,24,768]{2,1,0:T(8,128)(2,1)} %bitcast.15, bf16[50,24,768]{2,1,0:T(8,128)(2,1)} %bitcast.4.recv, f32[16,768]{1,0:T(8,128)} %get-tuple-element.193.extra), custom_call_target="tpu_custom_call" | custom-call | flops 1000000000 | bytes 1000000 | tf_op jit(solution)/shard_map/combine0/pallas_call | solution.py:765
  105.8 1.7 collective-permute-start.13
  107.5 15.8 %attn_bwd0.1 = (f32[192,4096]{1,0:T(8,128)}, f32[576,192]{1,0:T(8,128)}, f32[8,576]{1,0:T(8,128)}) custom-call(s32[1]{0:T(128)} %bitcast.me.refs_0_, s32[1]{0:T(128)} %bitcast.2.index.refs_1_, s32[16]{0:T(128)} %refs_2_.5, s32[4]{0:T(128)} %refs_3_.5, bf16[192,4096]{1,0:T(8,128)(2,1)} %refs_4_.7, bf16[192,576]{1,0:T(8,128)(2,1)} %bitcast.13, ...), custom_call_target="tpu_custom_call" | custom-call | flops 20000000000 | bytes 20000000 | tf_op jit(solution)/shard_map/attn_bwd0/pallas_call | solution.py:351
  123.3 6.3 %collective-permute-done.13.recv = bf16[26,24,768]{2,1,0:T(8,128)(2,1)} collective-permute-done((bf16[26,24,768]{2,1,0:T(8,128)(2,1)}, bf16[26,24,768]{2,1,0:T(8,128)(2,1)}, u32[]{:S(2)}, u32[]{:S(2)}) %collective-permute-start.13) | collective-permute-done | bytes 958496 | tf_op jit(solution)/shard_map/ppermute | solution.py:941
  129.6 2.5 %combine1.1 = (bf16[12,24,768]{2,1,0:T(8,128)(2,1)}, bf16[14,24,768]{2,1,0:T(8,128)(2,1)}, f32[16,768]{1,0:T(8,128)}) custom-call(s32[1]{0:T(128)} %constant.28.clone.1.index, bf16[24,24,768]{2,1,0:T(8,128)(2,1)} %get-tuple-element.196.keep, bf16[26,24,768]{2,1,0:T(8,128)(2,1)} %collective-permute-done.13.recv, f32[16,768]{1,0:T(8,128)} %get-tuple-element.209.extra), custom_call_target="tpu_custom_call" | custom-call | flops 1000000000 | bytes 1000000 | tf_op jit(solution)/shard_map/combine1/pallas_call | solution.py:765
  132.2 1.7 collective-permute-start.17
  133.9 11.8 %attn_bwd5.1 = (f32[192,4096]{1,0:T(8,128)}, bf16[4,72,192]{2,1,0:T(8,128)(2,1)}, bf16[5,72,192]{2,1,0:T(8,128)(2,1)}, f32[24,192]{1,0:T(8,128)}) custom-call(s32[1]{0:T(128)} %bitcast.me.refs_0_, s32[1]{0:T(128)} %bitcast.2.index.refs_1_, s32[16]{0:T(128)} %refs_2_.5, s32[4]{0:T(128)} %refs_3_.5, ...), custom_call_target="tpu_custom_call", output_to_operand_aliasing={{0}: (13, {})} | custom-call | flops 12000000000 | bytes 12000000 | tf_op jit(solution)/shard_map/attn_bwd5/pallas_call | solution.py:351
  145.7 1.7 collective-permute-start.18
  150.6 1.6 collective-permute-start.19
  153.6 6.0 %collective-permute-done.19.wr = bf16[8,24,768]{2,1,0:T(8,128)(2,1)S(1)} collective-permute-done((bf16[8,24,768]{2,1,0:T(8,128)(2,1)S(1)}, bf16[8,24,768]{2,1,0:T(8,128)(2,1)S(1)}, u32[]{:S(2)}, u32[]{:S(2)}) %collective-permute-start.19) | collective-permute-done | bytes 294944 | tf_op jit(solution)/shard_map/ppermute | solution.py:941
  160.9 2.7 %collective-permute-start.21 = (bf16[5,24,768]{2,1,0:T(8,128)(2,1)S(1)}, bf16[5,24,768]{2,1,0:T(8,128)(2,1)S(1)}, u32[]{:S(2)}, u32[]{:S(2)}) collective-permute-start(bf16[5,24,768]{2,1,0:T(8,128)(2,1)S(1)} %get-tuple-element.239), channel_id=1, source_target_pairs={{0,16},{4,20},{8,24},{12,28},{16,0},{20,4},{24,8},{28,12},{1,17},{... | collective-permute-start | bytes 552968 | tf_op jit(solution)/shard_map/ppermute | solution.py:941
  163.6 6.7 %collective-permute-done.21.wr = bf16[5,24,768]{2,1,0:T(8,128)(2,1)S(1)} collective-permute-done((bf16[5,24,768]{2,1,0:T(8,128)(2,1)S(1)}, bf16[5,24,768]{2,1,0:T(8,128)(2,1)S(1)}, u32[]{:S(2)}, u32[]{:S(2)}) %collective-permute-start.21) | collective-permute-done | bytes 184352 | tf_op jit(solution)/shard_map/ppermute | solution.py:941
  (42 shorter events, 11.4 us)
Async XLA Ops:
  2.8 23.5 %collective-permute-start = (bf16[592,768]{1,0:T(8,128)(2,1)}, bf16[592,768]{1,0:T(8,128)(2,1)}, u32[]{:S(2)}, u32[]{:S(2)}) collective-permute-start(bf16[592,768]{1,0:T(8,128)(2,1)} %pack.1.w0), channel_id=1, source_target_pairs={{0,2},{1,3},{2,0},{3,1},{4,6},{5,7},{6,4},{7,5},{8,10},{9,11},{10,... | collective-permute-start | bytes 2727944 | tf_op jit(solution)/shard_map/ppermute | solution.py:941
  5.7 20.5 %collective-permute-start.1 = (bf16[592,768]{1,0:T(8,128)(2,1)}, bf16[592,768]{1,0:T(8,128)(2,1)}, u32[]{:S(2)}, u32[]{:S(2)}) collective-permute-start(bf16[592,768]{1,0:T(8,128)(2,1)} %pack.1.w0), channel_id=1, source_target_pairs={{0,1},{1,0},{2,3},{3,2},{4,5},{5,4},{6,7},{7,6},{8,9},{9,8},{10,11... | collective-permute-start | bytes 2727944 | tf_op jit(solution)/shard_map/ppermute | solution.py:941
  26.2 2.8 %collective-permute-start.5 = (bf16[592,768]{1,0:T(8,128)(2,1)}, bf16[592,768]{1,0:T(8,128)(2,1)}, u32[]{:S(2)}, u32[]{:S(2)}) collective-permute-start(bf16[592,768]{1,0:T(8,128)(2,1)} %collective-permute-done.w2), channel_id=1, source_target_pairs={{0,1},{1,0},{2,3},{3,2},{4,5},{5,4},{6,7},{7,6},{8,9},{9,8},{10,11... | collective-permute-start | bytes 2727944 | tf_op jit(solution)/shard_map/ppermute | solution.py:941
  26.2 13.9 %collective-permute-start.2 = (bf16[2,192,512]{2,1,0:T(8,128)(2,1)}, bf16[2,192,512]{2,1,0:T(8,128)(2,1)}, u32[]{:S(2)}, u32[]{:S(2)}) collective-permute-start(bf16[2,192,512]{2,1,0:T(8,128)(2,1)} %get-tuple-element.144), channel_id=1, source_target_pairs={{0,1},{1,0},{2,3},{3,2},{4,5},{5,4},{6,7},{7,6},{8,9},{9,8},{10,11... | collective-permute-start | bytes 1179656 | tf_op jit(solution)/shard_map/ppermute | solution.py:941
  26.7 13.5 %collective-permute-start.3 = (bf16[2,192,512]{2,1,0:T(8,128)(2,1)}, bf16[2,192,512]{2,1,0:T(8,128)(2,1)}, u32[]{:S(2)}, u32[]{:S(2)}) collective-permute-start(bf16[2,192,512]{2,1,0:T(8,128)(2,1)} %get-tuple-element.145), channel_id=1, source_target_pairs={{0,2},{1,3},{2,0},{3,1},{4,6},{5,7},{6,4},{7,5},{8,10},{9,11},{10,... | collective-permute-start | bytes 1179656 | tf_op jit(solution)/shard_map/ppermute | solution.py:941
  28.5 18.2 %collective-permute-start.4 = (bf16[2,192,512]{2,1,0:T(8,128)(2,1)}, bf16[2,192,512]{2,1,0:T(8,128)(2,1)}, u32[]{:S(2)}, u32[]{:S(2)}) collective-permute-start(bf16[2,192,512]{2,1,0:T(8,128)(2,1)} %get-tuple-element.146), channel_id=1, source_target_pairs={{0,3},{1,2},{2,1},{3,0},{4,7},{5,6},{6,5},{7,4},{8,11},{9,10},{10,... | collective-permute-start | bytes 1179656 | tf_op jit(solution)/shard_map/ppermute | solution.py:941
  28.5 41.6 %collective-permute-start.6 = (bf16[2,192,512]{2,1,0:T(8,128)(2,1)}, bf16[2,192,512]{2,1,0:T(8,128)(2,1)}, u32[]{:S(2)}, u32[]{:S(2)}) collective-permute-start(bf16[2,192,512]{2,1,0:T(8,128)(2,1)} %get-tuple-element.167), channel_id=1, source_target_pairs={{0,1},{1,0},{2,3},{3,2},{4,5},{5,4},{6,7},{7,6},{8,9},{9,8},{10,11... | collective-permute-start | bytes 1179656 | tf_op jit(solution)/shard_map/ppermute | solution.py:941
  29.0 41.1 %collective-permute-start.7 = (bf16[2,192,512]{2,1,0:T(8,128)(2,1)}, bf16[2,192,512]{2,1,0:T(8,128)(2,1)}, u32[]{:S(2)}, u32[]{:S(2)}) collective-permute-start(bf16[2,192,512]{2,1,0:T(8,128)(2,1)} %get-tuple-element.168), channel_id=1, source_target_pairs={{0,2},{1,3},{2,0},{3,1},{4,6},{5,7},{6,4},{7,5},{8,10},{9,11},{10,... | collective-permute-start | bytes 1179656 | tf_op jit(solution)/shard_map/ppermute | solution.py:941
  40.2 30.0 %collective-permute-start.8 = (bf16[2,192,512]{2,1,0:T(8,128)(2,1)}, bf16[2,192,512]{2,1,0:T(8,128)(2,1)}, u32[]{:S(2)}, u32[]{:S(2)}) collective-permute-start(bf16[2,192,512]{2,1,0:T(8,128)(2,1)} %get-tuple-element.169), channel_id=1, source_target_pairs={{0,3},{1,2},{2,1},{3,0},{4,7},{5,6},{6,5},{7,4},{8,11},{9,10},{10,... | collective-permute-start | bytes 1179656 | tf_op jit(solution)/shard_map/ppermute | solution.py:941
  70.1 27.9 %collective-permute-start.10 = (bf16[2,192,512]{2,1,0:T(8,128)(2,1)}, bf16[2,192,512]{2,1,0:T(8,128)(2,1)}, u32[]{:S(2)}, u32[]{:S(2)}) collective-permute-start(bf16[2,192,512]{2,1,0:T(8,128)(2,1)} %get-tuple-element.189), channel_id=1, source_target_pairs={{0,2},{1,3},{2,0},{3,1},{4,6},{5,7},{6,4},{7,5},{8,10},{9,11},{10,... | collective-permute-start | bytes 1179656 | tf_op jit(solution)/shard_map/ppermute | solution.py:941
  70.8 27.3 %collective-permute-start.11 = (bf16[2,192,512]{2,1,0:T(8,128)(2,1)}, bf16[2,192,512]{2,1,0:T(8,128)(2,1)}, u32[]{:S(2)}, u32[]{:S(2)}) collective-permute-start(bf16[2,192,512]{2,1,0:T(8,128)(2,1)} %get-tuple-element.190), channel_id=1, source_target_pairs={{0,3},{1,2},{2,1},{3,0},{4,7},{5,6},{6,5},{7,4},{8,11},{9,10},{10,... | collective-permute-start | bytes 1179656 | tf_op jit(solution)/shard_map/ppermute | solution.py:941
  72.2 25.9 %collective-permute-start.9 = (bf16[2,192,512]{2,1,0:T(8,128)(2,1)}, bf16[2,192,512]{2,1,0:T(8,128)(2,1)}, u32[]{:S(2)}, u32[]{:S(2)}) collective-permute-start(bf16[2,192,512]{2,1,0:T(8,128)(2,1)} %get-tuple-element.188), channel_id=1, source_target_pairs={{0,1},{1,0},{2,3},{3,2},{4,5},{5,4},{6,7},{7,6},{8,9},{9,8},{10,11... | collective-permute-start | bytes 1179656 | tf_op jit(solution)/shard_map/ppermute | solution.py:941
  98.1 4.2 %collective-permute-start.12 = (bf16[1200,768]{1,0:T(8,128)(2,1)}, bf16[1200,768]{1,0:T(8,128)(2,1)}, u32[]{:S(2)}, u32[]{:S(2)}) collective-permute-start(bf16[1200,768]{1,0:T(8,128)(2,1)} %get-tuple-element.192), channel_id=1, source_target_pairs={{0,1},{1,0},{2,3},{3,2},{4,5},{5,4},{6,7},{7,6},{8,9},{9,8},{10,11... | collective-permute-start | bytes 5529608 | tf_op jit(solution)/shard_map/ppermute | solution.py:941
  98.5 35.3 %collective-permute-start.14 = (bf16[2,192,512]{2,1,0:T(8,128)(2,1)}, bf16[2,192,512]{2,1,0:T(8,128)(2,1)}, u32[]{:S(2)}, u32[]{:S(2)}) collective-permute-start(bf16[2,192,512]{2,1,0:T(8,128)(2,1)} %get-tuple-element.212), channel_id=1, source_target_pairs={{0,1},{1,0},{2,3},{3,2},{4,5},{5,4},{6,7},{7,6},{8,9},{9,8},{10,11... | collective-permute-start | bytes 1179656 | tf_op jit(solution)/shard_map/ppermute | solution.py:941
  98.7 35.1 %collective-permute-start.15 = (bf16[2,192,512]{2,1,0:T(8,128)(2,1)}, bf16[2,192,512]{2,1,0:T(8,128)(2,1)}, u32[]{:S(2)}, u32[]{:S(2)}) collective-permute-start(bf16[2,192,512]{2,1,0:T(8,128)(2,1)} %get-tuple-element.213), channel_id=1, source_target_pairs={{0,2},{1,3},{2,0},{3,1},{4,6},{5,7},{6,4},{7,5},{8,10},{9,11},{10,... | collective-permute-start | bytes 1179656 | tf_op jit(solution)/shard_map/ppermute | solution.py:941
  100.3 33.5 %collective-permute-start.16 = (bf16[2,192,512]{2,1,0:T(8,128)(2,1)}, bf16[2,192,512]{2,1,0:T(8,128)(2,1)}, u32[]{:S(2)}, u32[]{:S(2)}) collective-permute-start(bf16[2,192,512]{2,1,0:T(8,128)(2,1)} %get-tuple-element.214), channel_id=1, source_target_pairs={{0,3},{1,2},{2,1},{3,0},{4,7},{5,6},{6,5},{7,4},{8,11},{9,10},{10,... | collective-permute-start | bytes 1179656 | tf_op jit(solution)/shard_map/ppermute | solution.py:941
  105.8 23.8 %collective-permute-start.13 = (bf16[26,24,768]{2,1,0:T(8,128)(2,1)}, bf16[26,24,768]{2,1,0:T(8,128)(2,1)}, u32[]{:S(2)}, u32[]{:S(2)}) collective-permute-start(bf16[26,24,768]{2,1,0:T(8,128)(2,1)} %get-tuple-element.197), channel_id=1, source_target_pairs={{0,4},{4,0},{8,12},{12,8},{16,20},{20,16},{24,28},{28,24},{1,5},{5... | collective-permute-start | bytes 2875400 | tf_op jit(solution)/shard_map/ppermute | solution.py:941
  132.2 13.5 %collective-permute-start.17 = (bf16[14,24,768]{2,1,0:T(8,128)(2,1)}, bf16[14,24,768]{2,1,0:T(8,128)(2,1)}, u32[]{:S(2)}, u32[]{:S(2)}) collective-permute-start(bf16[14,24,768]{2,1,0:T(8,128)(2,1)} %get-tuple-element.219), channel_id=1, source_target_pairs={{0,2},{1,3},{2,0},{3,1},{4,6},{5,7},{6,4},{7,5},{8,10},{9,11},{10,... | collective-permute-start | bytes 1548296 | tf_op jit(solution)/shard_map/ppermute | solution.py:941
  145.7 6.6 %collective-permute-start.18 = (bf16[5,72,192]{2,1,0:T(8,128)(2,1)}, bf16[5,72,192]{2,1,0:T(8,128)(2,1)S(1)}, u32[]{:S(2)}, u32[]{:S(2)}) collective-permute-start(bf16[5,72,192]{2,1,0:T(8,128)(2,1)} %get-tuple-element.222), channel_id=1, source_target_pairs={{0,4},{4,0},{8,12},{12,8},{16,20},{20,16},{24,28},{28,24},{1,5},{5... | collective-permute-start | bytes 414728 | tf_op jit(solution)/shard_map/ppermute | solution.py:941
  149.2 3.1 %copy-start.2 = (bf16[4,72,192]{2,1,0:T(8,128)(2,1)S(1)}, bf16[4,72,192]{2,1,0:T(8,128)(2,1)}, u32[]{:S(2)}) copy-start(bf16[4,72,192]{2,1,0:T(8,128)(2,1)} %get-tuple-element.229.refs_0_) | copy-start | bytes 331780
  149.2 3.1 %copy-start.3 = (f32[24,192]{1,0:T(8,128)S(1)}, f32[24,192]{1,0:T(8,128)}, u32[]{:S(2)}) copy-start(f32[24,192]{1,0:T(8,128)} %get-tuple-element.230.refs_1_) | copy-start | bytes 55300
  150.6 9.0 %collective-permute-start.19 = (bf16[8,24,768]{2,1,0:T(8,128)(2,1)S(1)}, bf16[8,24,768]{2,1,0:T(8,128)(2,1)S(1)}, u32[]{:S(2)}, u32[]{:S(2)}) collective-permute-start(bf16[8,24,768]{2,1,0:T(8,128)(2,1)S(1)} %get-tuple-element.228), channel_id=1, source_target_pairs={{0,8},{4,12},{8,0},{12,4},{16,24},{20,28},{24,16},{28,20},{1,9},{5... | collective-permute-start | bytes 884744 | tf_op jit(solution)/shard_map/ppermute | solution.py:941
  152.6 8.2 %collective-permute-start.20 = (bf16[3,72,192]{2,1,0:T(8,128)(2,1)S(1)}, bf16[3,72,192]{2,1,0:T(8,128)(2,1)S(1)}, u32[]{:S(2)}, u32[]{:S(2)}) collective-permute-start(bf16[3,72,192]{2,1,0:T(8,128)(2,1)S(1)} %get-tuple-element.236), channel_id=1, source_target_pairs={{0,8},{4,12},{8,0},{12,4},{16,24},{20,28},{24,16},{28,20},{1,9},{5... | collective-permute-start | bytes 248840 | tf_op jit(solution)/shard_map/ppermute | solution.py:941
  160.9 9.4 %collective-permute-start.21 = (bf16[5,24,768]{2,1,0:T(8,128)(2,1)S(1)}, bf16[5,24,768]{2,1,0:T(8,128)(2,1)S(1)}, u32[]{:S(2)}, u32[]{:S(2)}) collective-permute-start(bf16[5,24,768]{2,1,0:T(8,128)(2,1)S(1)} %get-tuple-element.239), channel_id=1, source_target_pairs={{0,16},{4,20},{8,24},{12,28},{16,0},{20,4},{24,8},{28,12},{1,17},{... | collective-permute-start | bytes 552968 | tf_op jit(solution)/shard_map/ppermute | solution.py:941
  (2 other events, 1.8 us)

commit v2 on v1

--- a/solution.py
+++ b/solution.py
@@ -738,56 +738,113 @@
     )(me, *args)
 
 
-def combine_kernel(size, outer, inner, index, keep, recv, extra, kept, sent, extra_out):
-    rows = extra.shape[0]
-    more = extra[...] + (recv[size, :rows].astype(F32) + recv[size + 1, :rows].astype(F32))
+def put_pair(ref, at, value):
+    rows = value.shape[0]
+    high = value.astype(BF16)
+    ref[at, :rows] = high
+    ref[at + 1, :rows] = (value - high.astype(F32)).astype(BF16)
+
+
+def get_pair(ref, at, rows):
+    return ref[at, :rows].astype(F32) + ref[at + 1, :rows].astype(F32)
+
+
+def split_kernel(bit0, bit1, keep, recv, extra, kept, sent_y, sent_z, extra_out):
+    size = keep.shape[0]
+    per = size // 6
+    half = per // 2
+    more = extra[...] + get_pair(recv, size, extra.shape[0])
     extra_out[...] = more
-    hi = more.astype(BF16)
-    sent[size // 2, :rows] = hi
-    sent[size // 2 + 1, :rows] = (more - hi.astype(F32)).astype(BF16)
-    mine = index[0]
-    for o in range(outer):
-        a = pl.ds((o * 2 + mine) * inner, inner)
-        b = pl.ds((o * 2 + 1 - mine) * inner, inner)
-        c = slice(o * inner, (o + 1) * inner)
-        kept[c] = (keep[a].astype(F32) + recv[a].astype(F32)).astype(BF16)
-        sent[c] = (keep[b].astype(F32) + recv[b].astype(F32)).astype(BF16)
-
-
-def combine(index, keep, recv, extra, outer, inner, name):
-    size, rows, lanes = keep.shape
+    put_pair(sent_y, 4 * half, more)
+    low, high = bit0[0], bit1[0]
+
+    def total(i):
+        return (keep[i].astype(F32) + recv[i].astype(F32)).astype(BF16)
+
+    for k in range(2):
+        for section in range(3):
+            base = (k * 3 + section) * per
+            for e in range(half):
+                if section < 2:
+                    mine, other = base + 2 * e + low, base + 2 * e + 1 - low
+                    dest, at = sent_y, (k * 2 + section) * half + e
+                else:
+                    first = base + 4 * (e // 2) + e % 2
+                    mine, other = first + 2 * high, first + 2 * (1 - high)
+                    dest, at = sent_z, k * half + e
+                kept[base // 2 + e] = total(mine)
+                dest[at] = total(other)
+
+
+def join_kernel(keep, recv_y, recv_z, extra, kept, sent, extra_out):
+    half = keep.shape[0] // 6
+    more = extra[...] + get_pair(recv_y, 4 * half, extra.shape[0])
+    extra_out[...] = more
+    put_pair(sent, 3 * half, more)
+    for k in range(2):
+        for section in range(3):
+            for e in range(half):
+                if section < 2:
+                    other = recv_y[(k * 2 + section) * half + e]
+                else:
+                    other = recv_z[k * half + e]
+                value = keep[(k * 3 + section) * half + e].astype(F32) + other.astype(F32)
+                (sent if k else kept)[section * half + e] = value.astype(BF16)
+
+
+def early_kernel(bit0, bit1, keep, recv, extra, kept, sent_z, sent_y, extra_out):
+    size = keep.shape[0]
+    half = size // 6
+    more = extra[...] + get_pair(recv, size, extra.shape[0])
+    extra_out[...] = more
+    put_pair(sent_z, 2 * half, more)
+
+    def total(i):
+        return (keep[i].astype(F32) + recv[i].astype(F32)).astype(BF16)
+
+    for section in range(3):
+        mine = bit1[0] if section < 2 else bit0[0]
+        for e in range(half):
+            at = section * 2 * half + 2 * e
+            kept[section * half + e] = total(at + mine)
+            if section < 2:
+                sent_z[section * half + e] = total(at + 1 - mine)
+            else:
+                sent_y[e] = total(at + 1 - mine)
+
+
+def combine(kernel, bits, args, sizes, name):
+    rows, lanes = args[0].shape[1:]
     vmem = pl.BlockSpec(memory_space=pltpu.VMEM)
-    shapes = [
-        jax.ShapeDtypeStruct((size // 2, rows, lanes), BF16),
-        jax.ShapeDtypeStruct((size // 2 + 2, rows, lanes), BF16),
-        jax.ShapeDtypeStruct(extra.shape, F32),
-    ]
+    shapes = [jax.ShapeDtypeStruct((n, rows, lanes), BF16) for n in sizes]
+    shapes.append(jax.ShapeDtypeStruct(args[-1].shape, F32))
     return pl.pallas_call(
-        functools.partial(combine_kernel, size, outer, inner),
-        in_specs=[pl.BlockSpec(memory_space=pltpu.SMEM)] + [vmem] * 3,
+        kernel,
+        in_specs=[pl.BlockSpec(memory_space=pltpu.SMEM)] * len(bits) + [vmem] * len(args),
         out_specs=[vmem] * len(shapes),
         out_shape=shapes,
         cost_estimate=COST(1.0),
         compiler_params=pltpu.CompilerParams(vmem_limit_bytes=VMEM_LIMIT),
         name=name,
-    )(index, keep, recv, extra)
-
-
-def pulled(kernel, count, index, *refs):
+    )(*bits, *args)
+
+
+def pulled(kernel, bits, count, *refs):
+    bits, refs = refs[:bits], refs[bits:]
     bufs, sem = refs[-count - 1 : -1], refs[-1]
     copies = [pltpu.make_async_copy(refs[i], bufs[i], sem.at[i]) for i in range(count)]
     for c in copies:
         c.start()
     for c in copies:
         c.wait()
-    kernel(index, *bufs, *refs[count : -count - 1])
-
-
-def pull_call(kernel, count, index, args, shapes, name):
+    kernel(*bits, *bufs, *refs[count : -count - 1])
+
+
+def pull_call(kernel, count, bits, args, shapes, name):
     vmem = pl.BlockSpec(memory_space=pltpu.VMEM)
     return pl.pallas_call(
-        functools.partial(pulled, kernel, count),
-        in_specs=[pl.BlockSpec(memory_space=pltpu.SMEM)]
+        functools.partial(pulled, kernel, len(bits), count),
+        in_specs=[pl.BlockSpec(memory_space=pltpu.SMEM)] * len(bits)
         + [pl.BlockSpec(memory_space=pltpu.HBM)] * count
         + [vmem] * (len(args) - count),
         out_specs=[vmem] * len(shapes),
@@ -797,18 +854,19 @@
         cost_estimate=COST(1.0),
         compiler_params=pltpu.CompilerParams(vmem_limit_bytes=VMEM_SMALL),
         name=name,
-    )(index, *args)
-
-
-def combine_early(index, keep, recv, extra, name):
+    )(*bits, *args)
+
+
+def combine_early(bits, keep, recv, extra, name):
     size, rows, lanes = keep.shape
+    half = size // 6
     shapes = [
-        jax.ShapeDtypeStruct((size // 2, rows, lanes), BF16),
-        jax.ShapeDtypeStruct((size // 2 + 2, rows, lanes), BF16),
+        jax.ShapeDtypeStruct((3 * half, rows, lanes), BF16),
+        jax.ShapeDtypeStruct((2 * half + 2, rows, lanes), BF16),
+        jax.ShapeDtypeStruct((half, rows, lanes), BF16),
         jax.ShapeDtypeStruct(extra.shape, F32),
     ]
-    kernel = functools.partial(combine_kernel, size, size // 2, 1)
-    return pull_call(kernel, 3, index, [keep, recv, extra], shapes, name)
+    return pull_call(early_kernel, 3, bits, [keep, recv, extra], shapes, name)
 
 
 def qkv_kernel(index, qk, qb, qr, kept, sent, qb_out):
@@ -832,12 +890,12 @@
         jax.ShapeDtypeStruct((size // 2 + 1, rows, lanes), BF16),
         jax.ShapeDtypeStruct(qb.shape, F32),
     ]
-    return pull_call(qkv_kernel, 2, index, [qk, qb, qr], shapes, name)
+    return pull_call(qkv_kernel, 2, [index], [qk, qb, qr], shapes, name)
 
 
 def blend_kernel(joint, last, index, wk, wr, vec, qk, *refs):
     if not joint:
-        qr, qb, refs = refs[0], refs[1], refs[2:]
+        wy, qr, qb, refs = refs[0], refs[1], refs[2], refs[3:]
     nw, rows, model = wk.shape
     nq, width = qk.shape[0], qk.shape[2]
     pitch = model // 3
@@ -845,11 +903,13 @@
         terms = wr[nw].astype(F32)
         more = vec[:12] + (terms[:12] + terms[12:24])
     else:
-        more = vec[:12] + (wr[nw, :16].astype(F32) + wr[nw + 1, :16].astype(F32))[:12]
+        more = vec[:12] + get_pair(wr, wr.shape[0] - 2, 16)[:12]
         bias = qb[...] + (qr[nq, :24].astype(F32) + qr[nq, 24:48].astype(F32))
 
-    def wsum(i):
-        return wk[i].astype(F32) + wr[i].astype(F32)
+    def wsum(section, i):
+        at = section * (nw // 3) + i
+        other = wr[at] if joint or section < 2 else wy[i]
+        return wk[at].astype(F32) + other.astype(F32)
 
     def qsum(i, j):
         part = slice(j * rows, (j + 1) * rows)
@@ -862,9 +922,9 @@
     if last:
         gup, gdn, gow, gqkv, gqv, gub = refs[:6]
         vecs = refs[6:]
-        gup[...] = wsum(0)
-        gdn[...] = wsum(1)
-        ow = wsum(2)
+        gup[...] = wsum(0, 0)
+        gdn[...] = wsum(1, 0)
+        ow = wsum(2, 0)
         quarter = model // 4
         gow[...] = jnp.concatenate(
             [ow[:, j * quarter : (j + 1) * quarter] for j in range(4)], axis=0
@@ -892,9 +952,9 @@
     more = vec_out[:12]
     hi = more.astype(BF16).astype(F32)
     sent[half, :24] = jnp.concatenate([hi, more - hi], axis=0).astype(BF16)
-    for i in range(half):
-        wkept[i] = wsum(2 * i + mine).astype(BF16)
-        sent[i] = wsum(2 * i + 1 - mine).astype(BF16)
+    for i in range(3):
+        wkept[i] = wsum(i, mine).astype(BF16)
+        sent[i] = wsum(i, 1 - mine).astype(BF16)
     at = half + 1
     for i in range(nq // 2):
         for j in range(3):
@@ -902,11 +962,11 @@
             sent[at + i, :, j * pitch : j * pitch + width] = qsum(2 * i + 1 - mine, j).astype(BF16)
 
 
-def blend(index, wk, wr, vec, qk, qr, qb, last, name):
+def blend(index, wk, wr, wy, vec, qk, qr, qb, last, name):
     nw, rows, model = wk.shape
     nq, _, width = qk.shape
     vmem = pl.BlockSpec(memory_space=pltpu.VMEM)
-    args = [wk, wr, vec, qk] + ([] if qr is None else [qr, qb])
+    args = [wk, wr, vec, qk] + ([] if qr is None else [wy, qr, qb])
     shape = jax.ShapeDtypeStruct
     if last:
         quarter = model // 4
@@ -1053,7 +1113,7 @@
     dp = lax.axis_index("dp").astype(jnp.int32)
     me = chan[None]
     bar = lax.optimization_barrier
-    fine = width // dp_count >= 16 and dp_count >= 8
+    fine = width // dp_count >= 16 and dp_count == 8
     lengths = (lengths_short, lengths_long)
     w = qkv_weight[0]
 
@@ -1115,40 +1175,35 @@
     else:
         rows = width // dp_count
         size = 6 * dp_count
-        zero = jnp.zeros((1,), jnp.int32)
         recv = recv.reshape(size + 2, rows, model)
         keep = keep.reshape(size, rows, model)
 
-        def stage(index, recv, chan_next, name):
-            size = keep.shape[0]
-            outer, inner = (1, size // 2) if chan_next else (size // 2, 1)
-            return combine(index, keep, recv, vec, outer, inner, name)
-
-        keep, send, vec = stage(parity, recv, False, "combine0")
-        recv = swap(send, "dp", 1)
+        bits = [parity, digit(dp, 1)]
+        keep, send_y, send_z, vec = combine(
+            split_kernel, bits, [keep, recv, vec], [24, 18, 8], "combine0"
+        )
+        recv_y, recv_z = swap(send_y, "dp", 1), swap(send_z, "dp", 2)
         x, keep = bar((hidden_in, keep))
         carry = backward(0, 5, x, None, 0)
-        recv, carry = bar((recv, carry))
-        keep, send, vec = stage(zero, recv, True, "combine1")
+        recv_y, recv_z, carry = bar((recv_y, recv_z, carry))
+        keep, send, vec = combine(
+            join_kernel, [], [keep, recv_y, recv_z, vec], [12, 14], "combine1"
+        )
         recv = swap(send, "chan", 2)
         x, keep = bar((x, keep))
         grad_input, gk, gs, gbias = backward(5, 3, x, carry, 2)
         recv, gk, gs = bar((recv, gk, gs))
         grecv = swap(gs, "dp", 1)
-        second = digit(dp, 1)
-        keep, send, vec = combine_early(second, keep, recv, vec, "combine2")
-        recv = swap(send, "dp", 2)
+        keep, send_z, send_y, vec = combine_early(bits, keep, recv, vec, "combine2")
+        recv_z, recv_y = swap(send_z, "dp", 2), swap(send_y, "dp", 1)
         grecv, keep = bar((grecv, keep))
-        gk, gs, gbias = qkv_stage(second, gk, gbias, grecv, "qkv2")
+        gk, gs, gbias = qkv_stage(bits[1], gk, gbias, grecv, "qkv2")
         grecv = swap(gs, "dp", 2)
-        recv, gk = bar((recv, gk))
-        b = 2
-        while b < dp_count.bit_length() - 1:
-            keep, send, vec, gk = blend(
-                digit(dp, b), keep, recv, vec, gk, grecv, gbias, False, f"blend{b}"
-            )
-            recv, grecv = swap(send, "dp", 1 << b), None
-            b += 1
+        recv_z, recv_y, gk = bar((recv_z, recv_y, gk))
+        keep, send, vec, gk = blend(
+            digit(dp, 2), keep, recv_z, recv_y, vec, gk, grecv, gbias, False, "blend2"
+        )
+        recv = swap(send, "dp", 4)
         index = jnp.stack(
             [
                 jnp.zeros_like(dp),
@@ -1157,7 +1212,7 @@
             ]
         )
         gup, gdn, gow, gq, gqv, gub, *mine = blend(
-            index, keep, recv, vec, gk, grecv, gbias, True, "blend"
+            index, keep, recv, None, vec, gk, None, None, True, "blend"
         )
     return (
         lo,

time: 172 us -> 167 us (0.971)
  waiting for transfers between devices: 34 us -> 27.4 us
    ppermute x22 -> x24, waiting for transfers between devices: 34 us -> 27.4 us  [swap(): return lax.ppermute(value, axis, [(i, i ^ bit) for i in range(count)])]
    ppermute x22 -> x24, starting transfers between devices: 22.4 us -> 23.3 us  [swap(): return lax.ppermute(value, axis, [(i, i ^ bit) for i in range(count)])]
  transfers between devices with their start and end apart: 22 -> 24, of which waited for: 8 -> 10; matrix products, arithmetic and copies ran while one was open for 0% -> 0% of each run, Pallas kernels for 63% -> 66%
where the time goes in v2:
time: 167 us; the launch traced here: 166 us
  Pallas kernels  113 us (68%)
  waiting for transfers between devices  27.4 us (16%)
  starting transfers between devices  23.3 us (14%)
  local copies, waits for them, and re-layouts  1.82 us (1%)
    pallas_call x2, Pallas kernels, mid(): pl.pallas_call(functools.partial(mid_kernel, half, width, blocks), grid_s...  49.1 us
    pallas_call x2, Pallas kernels, attn_bwd(): pl.pallas_call(functools.partial(attn_bwd_kernel, first, count, heads, sh...  27.7 us
    ppermute x24, waiting for transfers between devices, swap(): return lax.ppermute(value, axis, [(i, i ^ bit) for i in range(count)])  27.4 us
    ppermute x24, starting transfers between devices, swap(): return lax.ppermute(value, axis, [(i, i ^ bit) for i in range(count)])  23.3 us
    pallas_call x1, Pallas kernels, attn_fwd(): pl.pallas_call(functools.partial(attn_fwd_kernel, heads, short_blocks), g...  15.2 us
    pallas_call x1, Pallas kernels, prep(): pl.pallas_call(prep_kernel, in_specs=[vmem] * 10, out_specs=[vmem] * len(...  9.36 us
    pallas_call x2, Pallas kernels, combine(): pl.pallas_call(kernel, in_specs=[pl.BlockSpec(memory_space=pltpu.SMEM)] *...  5.94 us
  transfers between devices with their start and end apart: 24, of which 10 were waited for; matrix products, arithmetic and copies ran while one was open for 0% of the time, Pallas kernels for 66%

profile of v2, /device:TPU:0, one launch (start us, length us, event | category | flops | bytes accessed | tf_op | source)
XLA Modules:
  0.0 166.2 jit_solution(4762562220096461460)
XLA Ops:
  0.6 2.1 %pack.1.w0 = bf16[592,768]{1,0:T(8,128)(2,1)} custom-call(bf16[192,768]{1,0:T(8,128)(2,1)} %ow.1, bf16[192,768]{1,0:T(8,128)(2,1)} %up.1, bf16[192,768]{1,0:T(8,128)(2,1)} %dn.1, f32[768]{0:T(1024)} %ub.1), custom_call_target="tpu_custom_call" | custom-call | flops 1000000000 | bytes 1000000 | tf_op jit(solution)/shard_map/pack/pallas_call | solution.py:1057
  2.8 3.0 %collective-permute-start = (bf16[592,768]{1,0:T(8,128)(2,1)}, bf16[592,768]{1,0:T(8,128)(2,1)}, u32[]{:S(2)}, u32[]{:S(2)}) collective-permute-start(bf16[592,768]{1,0:T(8,128)(2,1)} %pack.1.w0), channel_id=1, source_target_pairs={{0,2},{1,3},{2,0},{3,1},{4,6},{5,7},{6,4},{7,5},{8,10},{9,11},{10,... | collective-permute-start | bytes 2727944 | tf_op jit(solution)/shard_map/ppermute | solution.py:1001
  5.7 15.2 %attn_fwd.1 = (bf16[8,576,512]{2,1,0:T(8,128)(2,1)}, bf16[1,192,512]{2,1,0:T(8,128)(2,1)}, bf16[2,192,512]{2,1,0:T(8,128)(2,1)}, bf16[2,192,512]{2,1,0:T(8,128)(...) custom-call(s32[1]{0:T(128)} %bitcast.me.refs_0_, ...), custom_call_target="tpu_custom_call" | custom-call | flops 16000000000 | bytes 16000000 | tf_op jit(solution)/shard_map/attn_fwd/pallas_call | solution.py:147
  21.0 5.2 %collective-permute-done.w2 = bf16[592,768]{1,0:T(8,128)(2,1)} collective-permute-done((bf16[592,768]{1,0:T(8,128)(2,1)}, bf16[592,768]{1,0:T(8,128)(2,1)}, u32[]{:S(2)}, u32[]{:S(2)}) %collective-permute-start) | collective-permute-done | bytes 909344 | tf_op jit(solution)/shard_map/ppermute | solution.py:1001
  26.7 1.7 %collective-permute-start.3 = (bf16[2,192,512]{2,1,0:T(8,128)(2,1)}, bf16[2,192,512]{2,1,0:T(8,128)(2,1)}, u32[]{:S(2)}, u32[]{:S(2)}) collective-permute-start(bf16[2,192,512]{2,1,0:T(8,128)(2,1)} %get-tuple-element.149), channel_id=1, source_target_pairs={{0,2},{1,3},{2,0},{3,1},{4,6},{5,7},{6,4},{7,5},{8,10},{9,11},{10,... | collective-permute-start | bytes 1179656 | tf_op jit(solution)/shard_map/ppermute | solution.py:1001
  29.0 1.7 %collective-permute-start.7 = (bf16[2,192,512]{2,1,0:T(8,128)(2,1)}, bf16[2,192,512]{2,1,0:T(8,128)(2,1)}, u32[]{:S(2)}, u32[]{:S(2)}) collective-permute-start(bf16[2,192,512]{2,1,0:T(8,128)(2,1)} %get-tuple-element.172), channel_id=1, source_target_pairs={{0,2},{1,3},{2,0},{3,1},{4,6},{5,7},{6,4},{7,5},{8,10},{9,11},{10,... | collective-permute-start | bytes 1179656 | tf_op jit(solution)/shard_map/ppermute | solution.py:1001
  30.8 9.4 %prep.1 = (bf16[768,768]{1,0:T(8,128)(2,1)}, bf16[4,768,192]{2,1,0:T(8,128)(2,1)}, bf16[4,768,192]{2,1,0:T(8,128)(2,1)}, bf16[4,192,768]{2,1,0:T(8,128)(2,1)}, b...) custom-call(bf16[592,768]{1,0:T(8,128)(2,1)} %pack.1.w0, ...), custom_call_target="tpu_custom_call" | custom-call | flops 4000000000 | bytes 4000000 | tf_op jit(solution)/shard_map/prep/pallas_call | solution.py:432
  40.2 6.5 %collective-permute-done.4.refs_3_.refs_7_ = bf16[2,192,512]{2,1,0:T(8,128)(2,1)} collective-permute-done((bf16[2,192,512]{2,1,0:T(8,128)(2,1)}, bf16[2,192,512]{2,1,0:T(8,128)(2,1)}, u32[]{:S(2)}, u32[]{:S(2)}) %collective-permute-start.4) | collective-permute-done | bytes 393248 | tf_op jit(solution)/shard_map/ppermute | solution.py:1001
  46.7 23.4 %mid0.1 = (bf16[1024,768]{1,0:T(8,128)(2,1)}, bf16[2,192,512]{2,1,0:T(8,128)(2,1)}, bf16[2,192,512]{2,1,0:T(8,128)(2,1)}, bf16[2,192,512]{2,1,0:T(8,128)(2,1)}, ...) custom-call(s32[1]{0:T(128)} %bitcast.me.refs_0_, ...), custom_call_target="tpu_custom_call" | custom-call | flops 24999999488 | bytes 25000000 | tf_op jit(solution)/shard_map/mid0/pallas_call | solution.py:723
  70.8 1.4 collective-permute-start.11
  72.4 25.7 %mid1.1 = (bf16[1024,768]{1,0:T(8,128)(2,1)}, bf16[2,192,512]{2,1,0:T(8,128)(2,1)}, bf16[2,192,512]{2,1,0:T(8,128)(2,1)}, bf16[2,192,512]{2,1,0:T(8,128)(2,1)}, ...) custom-call(s32[1]{0:T(128)} %bitcast.me.refs_0_, ...), custom_call_target="tpu_custom_call", output_to_operand_aliasing={{0}: (22, {})} | custom-call | flops 24999999488 | bytes 25000000 | tf_op jit(solution)/shard_map/mid1/pallas_call | solution.py:723
  98.7 1.6 collective-permute-start.16
  100.4 1.9 %collective-permute-done.12 = bf16[1200,768]{1,0:T(8,128)(2,1)} collective-permute-done((bf16[1200,768]{1,0:T(8,128)(2,1)}, bf16[1200,768]{1,0:T(8,128)(2,1)}, u32[]{:S(2)}, u32[]{:S(2)}) %collective-permute-start.12) | collective-permute-done | bytes 1843232 | tf_op jit(solution)/shard_map/ppermute | solution.py:1001
  102.3 3.4 %combine0.1 = (bf16[24,24,768]{2,1,0:T(8,128)(2,1)}, bf16[18,24,768]{2,1,0:T(8,128)(2,1)}, bf16[8,24,768]{2,1,0:T(8,128)(2,1)}, f32[16,768]{1,0:T(8,128)}) custom-call(s32[1]{0:T(128)} %bitcast.2.bit0.refs_1_.refs_0_, s32[1]{0:T(128)} %bitcast.3.bit1.refs_1_.refs_0_, bf16[48,24,768]{2,1,0:T(8,128)(2,1)} %bitcast.15, bf16[50,24,768]{2,1,0:T(8,128)(2,1)} %bitcast.5.recv, ...), custom_call_target="tpu_custom_call" | custom-call | flops 1000000000 | bytes 1000000 | tf_op jit(solution)/shard_map/combine0/pallas_call | solution.py:821
  105.8 1.7 collective-permute-start.13
  107.4 1.6 collective-permute-start.14
  109.0 15.9 %attn_bwd0.1 = (f32[192,4096]{1,0:T(8,128)}, f32[576,192]{1,0:T(8,128)}, f32[8,576]{1,0:T(8,128)}) custom-call(s32[1]{0:T(128)} %bitcast.me.refs_0_, s32[1]{0:T(128)} %bitcast.2.bit0.refs_1_.refs_0_, s32[16]{0:T(128)} %refs_2_.5, s32[4]{0:T(128)} %refs_3_.5, bf16[192,4096]{1,0:T(8,128)(2,1)} %refs_4_.7, bf16[192,576]{1,0:T(8,128)(2,1)} %bitcast.13, ...), custom_call_target="tpu_custom_call" | custom-call | flops 20000000000 | bytes 20000000 | tf_op jit(solution)/shard_map/attn_bwd0/pallas_call | solution.py:351
  124.9 2.5 %combine1.1 = (bf16[12,24,768]{2,1,0:T(8,128)(2,1)}, bf16[14,24,768]{2,1,0:T(8,128)(2,1)}, f32[16,768]{1,0:T(8,128)}) custom-call(bf16[24,24,768]{2,1,0:T(8,128)(2,1)} %get-tuple-element.200.keep, bf16[18,24,768]{2,1,0:T(8,128)(2,1)} %collective-permute-done.13.recv_y, bf16[8,24,768]{2,1,0:T(8,128)(2,1)} %collective-permute-done.14.recv_z, ...), custom_call_target="tpu_custom_call" | custom-call | flops 1000000000 | bytes 1000000 | tf_op jit(solution)/shard_map/combine1/pallas_call | solution.py:821
  127.4 2.9 %collective-permute-start.18 = (bf16[14,24,768]{2,1,0:T(8,128)(2,1)}, bf16[14,24,768]{2,1,0:T(8,128)(2,1)}, u32[]{:S(2)}, u32[]{:S(2)}) collective-permute-start(bf16[14,24,768]{2,1,0:T(8,128)(2,1)} %get-tuple-element.225), channel_id=1, source_target_pairs={{0,2},{1,3},{2,0},{3,1},{4,6},{5,7},{6,4},{7,5},{8,10},{9,11},{10,... | collective-permute-start | bytes 1548296 | tf_op jit(solution)/shard_map/ppermute | solution.py:1001
  130.3 11.8 %attn_bwd5.1 = (f32[192,4096]{1,0:T(8,128)}, bf16[4,72,192]{2,1,0:T(8,128)(2,1)}, bf16[5,72,192]{2,1,0:T(8,128)(2,1)}, f32[24,192]{1,0:T(8,128)}) custom-call(s32[1]{0:T(128)} %bitcast.me.refs_0_, s32[1]{0:T(128)} %bitcast.2.bit0.refs_1_.refs_0_, s32[16]{0:T(128)} %refs_2_.5, s32[4]{0:T(128)} %refs_3_.5, ...), custom_call_target="tpu_custom_call", output_to_operand_aliasing={{0}: (13, {})} | custom-call | flops 12000000000 | bytes 12000000 | tf_op jit(solution)/shard_map/attn_bwd5/pallas_call | solution.py:351
  146.5 1.9 %collective-permute-done.19.refs_3_ = bf16[5,72,192]{2,1,0:T(8,128)(2,1)S(1)} collective-permute-done((bf16[5,72,192]{2,1,0:T(8,128)(2,1)}, bf16[5,72,192]{2,1,0:T(8,128)(2,1)S(1)}, u32[]{:S(2)}, u32[]{:S(2)}) %collective-permute-start.19) | collective-permute-done | bytes 138272 | tf_op jit(solution)/shard_map/ppermute | solution.py:1001
  150.0 3.5 %collective-permute-done.21.refs_0_ = bf16[2,24,768]{2,1,0:T(8,128)(2,1)S(1)} collective-permute-done((bf16[2,24,768]{2,1,0:T(8,128)(2,1)S(1)}, bf16[2,24,768]{2,1,0:T(8,128)(2,1)S(1)}, u32[]{:S(2)}, u32[]{:S(2)}) %collective-permute-start.21) | collective-permute-done | bytes 73760 | tf_op jit(solution)/shard_map/ppermute | solution.py:1001
  155.0 2.9 %collective-permute-start.23 = (bf16[5,24,768]{2,1,0:T(8,128)(2,1)S(1)}, bf16[5,24,768]{2,1,0:T(8,128)(2,1)S(1)}, u32[]{:S(2)}, u32[]{:S(2)}) collective-permute-start(bf16[5,24,768]{2,1,0:T(8,128)(2,1)S(1)} %get-tuple-element.247), channel_id=1, source_target_pairs={{0,16},{4,20},{8,24},{12,28},{16,0},{20,4},{24,8},{28,12},{1,17},{... | collective-permute-start | bytes 552968 | tf_op jit(solution)/shard_map/ppermute | solution.py:1001
  158.0 6.7 %collective-permute-done.23.wr = bf16[5,24,768]{2,1,0:T(8,128)(2,1)S(1)} collective-permute-done((bf16[5,24,768]{2,1,0:T(8,128)(2,1)S(1)}, bf16[5,24,768]{2,1,0:T(8,128)(2,1)S(1)}, u32[]{:S(2)}, u32[]{:S(2)}) %collective-permute-start.23) | collective-permute-done | bytes 184352 | tf_op jit(solution)/shard_map/ppermute | solution.py:1001
  (46 shorter events, 11.6 us)
Async XLA Ops:
  2.8 23.5 %collective-permute-start = (bf16[592,768]{1,0:T(8,128)(2,1)}, bf16[592,768]{1,0:T(8,128)(2,1)}, u32[]{:S(2)}, u32[]{:S(2)}) collective-permute-start(bf16[592,768]{1,0:T(8,128)(2,1)} %pack.1.w0), channel_id=1, source_target_pairs={{0,2},{1,3},{2,0},{3,1},{4,6},{5,7},{6,4},{7,5},{8,10},{9,11},{10,... | collective-permute-start | bytes 2727944 | tf_op jit(solution)/shard_map/ppermute | solution.py:1001
  5.7 20.5 %collective-permute-start.1 = (bf16[592,768]{1,0:T(8,128)(2,1)}, bf16[592,768]{1,0:T(8,128)(2,1)}, u32[]{:S(2)}, u32[]{:S(2)}) collective-permute-start(bf16[592,768]{1,0:T(8,128)(2,1)} %pack.1.w0), channel_id=1, source_target_pairs={{0,1},{1,0},{2,3},{3,2},{4,5},{5,4},{6,7},{7,6},{8,9},{9,8},{10,11... | collective-permute-start | bytes 2727944 | tf_op jit(solution)/shard_map/ppermute | solution.py:1001
  26.2 2.8 %collective-permute-start.5 = (bf16[592,768]{1,0:T(8,128)(2,1)}, bf16[592,768]{1,0:T(8,128)(2,1)}, u32[]{:S(2)}, u32[]{:S(2)}) collective-permute-start(bf16[592,768]{1,0:T(8,128)(2,1)} %collective-permute-done.w2), channel_id=1, source_target_pairs={{0,1},{1,0},{2,3},{3,2},{4,5},{5,4},{6,7},{7,6},{8,9},{9,8},{10,11... | collective-permute-start | bytes 2727944 | tf_op jit(solution)/shard_map/ppermute | solution.py:1001
  26.2 13.9 %collective-permute-start.2 = (bf16[2,192,512]{2,1,0:T(8,128)(2,1)}, bf16[2,192,512]{2,1,0:T(8,128)(2,1)}, u32[]{:S(2)}, u32[]{:S(2)}) collective-permute-start(bf16[2,192,512]{2,1,0:T(8,128)(2,1)} %get-tuple-element.148), channel_id=1, source_target_pairs={{0,1},{1,0},{2,3},{3,2},{4,5},{5,4},{6,7},{7,6},{8,9},{9,8},{10,11... | collective-permute-start | bytes 1179656 | tf_op jit(solution)/shard_map/ppermute | solution.py:1001
  26.7 13.5 %collective-permute-start.3 = (bf16[2,192,512]{2,1,0:T(8,128)(2,1)}, bf16[2,192,512]{2,1,0:T(8,128)(2,1)}, u32[]{:S(2)}, u32[]{:S(2)}) collective-permute-start(bf16[2,192,512]{2,1,0:T(8,128)(2,1)} %get-tuple-element.149), channel_id=1, source_target_pairs={{0,2},{1,3},{2,0},{3,1},{4,6},{5,7},{6,4},{7,5},{8,10},{9,11},{10,... | collective-permute-start | bytes 1179656 | tf_op jit(solution)/shard_map/ppermute | solution.py:1001
  28.5 18.2 %collective-permute-start.4 = (bf16[2,192,512]{2,1,0:T(8,128)(2,1)}, bf16[2,192,512]{2,1,0:T(8,128)(2,1)}, u32[]{:S(2)}, u32[]{:S(2)}) collective-permute-start(bf16[2,192,512]{2,1,0:T(8,128)(2,1)} %get-tuple-element.150), channel_id=1, source_target_pairs={{0,3},{1,2},{2,1},{3,0},{4,7},{5,6},{6,5},{7,4},{8,11},{9,10},{10,... | collective-permute-start | bytes 1179656 | tf_op jit(solution)/shard_map/ppermute | solution.py:1001
  28.5 41.6 %collective-permute-start.6 = (bf16[2,192,512]{2,1,0:T(8,128)(2,1)}, bf16[2,192,512]{2,1,0:T(8,128)(2,1)}, u32[]{:S(2)}, u32[]{:S(2)}) collective-permute-start(bf16[2,192,512]{2,1,0:T(8,128)(2,1)} %get-tuple-element.171), channel_id=1, source_target_pairs={{0,1},{1,0},{2,3},{3,2},{4,5},{5,4},{6,7},{7,6},{8,9},{9,8},{10,11... | collective-permute-start | bytes 1179656 | tf_op jit(solution)/shard_map/ppermute | solution.py:1001
  29.0 41.1 %collective-permute-start.7 = (bf16[2,192,512]{2,1,0:T(8,128)(2,1)}, bf16[2,192,512]{2,1,0:T(8,128)(2,1)}, u32[]{:S(2)}, u32[]{:S(2)}) collective-permute-start(bf16[2,192,512]{2,1,0:T(8,128)(2,1)} %get-tuple-element.172), channel_id=1, source_target_pairs={{0,2},{1,3},{2,0},{3,1},{4,6},{5,7},{6,4},{7,5},{8,10},{9,11},{10,... | collective-permute-start | bytes 1179656 | tf_op jit(solution)/shard_map/ppermute | solution.py:1001
  40.2 30.0 %collective-permute-start.8 = (bf16[2,192,512]{2,1,0:T(8,128)(2,1)}, bf16[2,192,512]{2,1,0:T(8,128)(2,1)}, u32[]{:S(2)}, u32[]{:S(2)}) collective-permute-start(bf16[2,192,512]{2,1,0:T(8,128)(2,1)} %get-tuple-element.173), channel_id=1, source_target_pairs={{0,3},{1,2},{2,1},{3,0},{4,7},{5,6},{6,5},{7,4},{8,11},{9,10},{10,... | collective-permute-start | bytes 1179656 | tf_op jit(solution)/shard_map/ppermute | solution.py:1001
  70.1 27.9 %collective-permute-start.10 = (bf16[2,192,512]{2,1,0:T(8,128)(2,1)}, bf16[2,192,512]{2,1,0:T(8,128)(2,1)}, u32[]{:S(2)}, u32[]{:S(2)}) collective-permute-start(bf16[2,192,512]{2,1,0:T(8,128)(2,1)} %get-tuple-element.193), channel_id=1, source_target_pairs={{0,2},{1,3},{2,0},{3,1},{4,6},{5,7},{6,4},{7,5},{8,10},{9,11},{10,... | collective-permute-start | bytes 1179656 | tf_op jit(solution)/shard_map/ppermute | solution.py:1001
  70.8 27.3 %collective-permute-start.11 = (bf16[2,192,512]{2,1,0:T(8,128)(2,1)}, bf16[2,192,512]{2,1,0:T(8,128)(2,1)}, u32[]{:S(2)}, u32[]{:S(2)}) collective-permute-start(bf16[2,192,512]{2,1,0:T(8,128)(2,1)} %get-tuple-element.194), channel_id=1, source_target_pairs={{0,3},{1,2},{2,1},{3,0},{4,7},{5,6},{6,5},{7,4},{8,11},{9,10},{10,... | collective-permute-start | bytes 1179656 | tf_op jit(solution)/shard_map/ppermute | solution.py:1001
  72.2 25.9 %collective-permute-start.9 = (bf16[2,192,512]{2,1,0:T(8,128)(2,1)}, bf16[2,192,512]{2,1,0:T(8,128)(2,1)}, u32[]{:S(2)}, u32[]{:S(2)}) collective-permute-start(bf16[2,192,512]{2,1,0:T(8,128)(2,1)} %get-tuple-element.192), channel_id=1, source_target_pairs={{0,1},{1,0},{2,3},{3,2},{4,5},{5,4},{6,7},{7,6},{8,9},{9,8},{10,11... | collective-permute-start | bytes 1179656 | tf_op jit(solution)/shard_map/ppermute | solution.py:1001
  98.1 4.2 %collective-permute-start.12 = (bf16[1200,768]{1,0:T(8,128)(2,1)}, bf16[1200,768]{1,0:T(8,128)(2,1)}, u32[]{:S(2)}, u32[]{:S(2)}) collective-permute-start(bf16[1200,768]{1,0:T(8,128)(2,1)} %get-tuple-element.196), channel_id=1, source_target_pairs={{0,1},{1,0},{2,3},{3,2},{4,5},{5,4},{6,7},{7,6},{8,9},{9,8},{10,11... | collective-permute-start | bytes 5529608 | tf_op jit(solution)/shard_map/ppermute | solution.py:1001
  98.5 31.7 %collective-permute-start.15 = (bf16[2,192,512]{2,1,0:T(8,128)(2,1)}, bf16[2,192,512]{2,1,0:T(8,128)(2,1)}, u32[]{:S(2)}, u32[]{:S(2)}) collective-permute-start(bf16[2,192,512]{2,1,0:T(8,128)(2,1)} %get-tuple-element.218), channel_id=1, source_target_pairs={{0,1},{1,0},{2,3},{3,2},{4,5},{5,4},{6,7},{7,6},{8,9},{9,8},{10,11... | collective-permute-start | bytes 1179656 | tf_op jit(solution)/shard_map/ppermute | solution.py:1001
  98.7 31.6 %collective-permute-start.16 = (bf16[2,192,512]{2,1,0:T(8,128)(2,1)}, bf16[2,192,512]{2,1,0:T(8,128)(2,1)}, u32[]{:S(2)}, u32[]{:S(2)}) collective-permute-start(bf16[2,192,512]{2,1,0:T(8,128)(2,1)} %get-tuple-element.219), channel_id=1, source_target_pairs={{0,2},{1,3},{2,0},{3,1},{4,6},{5,7},{6,4},{7,5},{8,10},{9,11},{10,... | collective-permute-start | bytes 1179656 | tf_op jit(solution)/shard_map/ppermute | solution.py:1001
  100.3 30.0 %collective-permute-start.17 = (bf16[2,192,512]{2,1,0:T(8,128)(2,1)}, bf16[2,192,512]{2,1,0:T(8,128)(2,1)}, u32[]{:S(2)}, u32[]{:S(2)}) collective-permute-start(bf16[2,192,512]{2,1,0:T(8,128)(2,1)} %get-tuple-element.220), channel_id=1, source_target_pairs={{0,3},{1,2},{2,1},{3,0},{4,7},{5,6},{6,5},{7,4},{8,11},{9,10},{10,... | collective-permute-start | bytes 1179656 | tf_op jit(solution)/shard_map/ppermute | solution.py:1001
  105.8 19.1 %collective-permute-start.13 = (bf16[18,24,768]{2,1,0:T(8,128)(2,1)}, bf16[18,24,768]{2,1,0:T(8,128)(2,1)}, u32[]{:S(2)}, u32[]{:S(2)}) collective-permute-start(bf16[18,24,768]{2,1,0:T(8,128)(2,1)} %get-tuple-element.201), channel_id=1, source_target_pairs={{0,4},{4,0},{8,12},{12,8},{16,20},{20,16},{24,28},{28,24},{1,5},{5... | collective-permute-start | bytes 1990664 | tf_op jit(solution)/shard_map/ppermute | solution.py:1001
  107.4 17.4 %collective-permute-start.14 = (bf16[8,24,768]{2,1,0:T(8,128)(2,1)}, bf16[8,24,768]{2,1,0:T(8,128)(2,1)}, u32[]{:S(2)}, u32[]{:S(2)}) collective-permute-start(bf16[8,24,768]{2,1,0:T(8,128)(2,1)} %get-tuple-element.202), channel_id=1, source_target_pairs={{0,8},{4,12},{8,0},{12,4},{16,24},{20,28},{24,16},{28,20},{1,9},{5... | collective-permute-start | bytes 884744 | tf_op jit(solution)/shard_map/ppermute | solution.py:1001
  127.4 14.9 %collective-permute-start.18 = (bf16[14,24,768]{2,1,0:T(8,128)(2,1)}, bf16[14,24,768]{2,1,0:T(8,128)(2,1)}, u32[]{:S(2)}, u32[]{:S(2)}) collective-permute-start(bf16[14,24,768]{2,1,0:T(8,128)(2,1)} %get-tuple-element.225), channel_id=1, source_target_pairs={{0,2},{1,3},{2,0},{3,1},{4,6},{5,7},{6,4},{7,5},{8,10},{9,11},{10,... | collective-permute-start | bytes 1548296 | tf_op jit(solution)/shard_map/ppermute | solution.py:1001
  142.3 6.1 %collective-permute-start.19 = (bf16[5,72,192]{2,1,0:T(8,128)(2,1)}, bf16[5,72,192]{2,1,0:T(8,128)(2,1)S(1)}, u32[]{:S(2)}, u32[]{:S(2)}) collective-permute-start(bf16[5,72,192]{2,1,0:T(8,128)(2,1)} %get-tuple-element.228), channel_id=1, source_target_pairs={{0,4},{4,0},{8,12},{12,8},{16,20},{20,16},{24,28},{28,24},{1,5},{5... | collective-permute-start | bytes 414728 | tf_op jit(solution)/shard_map/ppermute | solution.py:1001
  146.0 7.7 %collective-permute-start.20 = (bf16[6,24,768]{2,1,0:T(8,128)(2,1)S(1)}, bf16[6,24,768]{2,1,0:T(8,128)(2,1)S(1)}, u32[]{:S(2)}, u32[]{:S(2)}) collective-permute-start(bf16[6,24,768]{2,1,0:T(8,128)(2,1)S(1)} %get-tuple-element.234), channel_id=1, source_target_pairs={{0,8},{4,12},{8,0},{12,4},{16,24},{20,28},{24,16},{28,20},{1,9},{5... | collective-permute-start | bytes 663560 | tf_op jit(solution)/shard_map/ppermute | solution.py:1001
  148.7 6.2 %collective-permute-start.22 = (bf16[3,72,192]{2,1,0:T(8,128)(2,1)S(1)}, bf16[3,72,192]{2,1,0:T(8,128)(2,1)S(1)}, u32[]{:S(2)}, u32[]{:S(2)}) collective-permute-start(bf16[3,72,192]{2,1,0:T(8,128)(2,1)S(1)} %get-tuple-element.244), channel_id=1, source_target_pairs={{0,8},{4,12},{8,0},{12,4},{16,24},{20,28},{24,16},{28,20},{1,9},{5... | collective-permute-start | bytes 248840 | tf_op jit(solution)/shard_map/ppermute | solution.py:1001
  149.2 4.4 %collective-permute-start.21 = (bf16[2,24,768]{2,1,0:T(8,128)(2,1)S(1)}, bf16[2,24,768]{2,1,0:T(8,128)(2,1)S(1)}, u32[]{:S(2)}, u32[]{:S(2)}) collective-permute-start(bf16[2,24,768]{2,1,0:T(8,128)(2,1)S(1)} %get-tuple-element.235), channel_id=1, source_target_pairs={{0,4},{4,0},{8,12},{12,8},{16,20},{20,16},{24,28},{28,24},{1,5},{5... | collective-permute-start | bytes 221192 | tf_op jit(solution)/shard_map/ppermute | solution.py:1001
  155.0 9.6 %collective-permute-start.23 = (bf16[5,24,768]{2,1,0:T(8,128)(2,1)S(1)}, bf16[5,24,768]{2,1,0:T(8,128)(2,1)S(1)}, u32[]{:S(2)}, u32[]{:S(2)}) collective-permute-start(bf16[5,24,768]{2,1,0:T(8,128)(2,1)S(1)} %get-tuple-element.247), channel_id=1, source_target_pairs={{0,16},{4,20},{8,24},{12,28},{16,0},{20,4},{24,8},{28,12},{1,17},{... | collective-permute-start | bytes 552968 | tf_op jit(solution)/shard_map/ppermute | solution.py:1001
  (4 other events, 9.4 us)

commit v3 on v2

--- a/solution.py
+++ b/solution.py
@@ -749,43 +749,73 @@
     return ref[at, :rows].astype(F32) + ref[at + 1, :rows].astype(F32)
 
 
-def split_kernel(bit0, bit1, keep, recv, extra, kept, sent_y, sent_z, extra_out):
-    size = keep.shape[0]
-    per = size // 6
+def split_kernel(bit0, bit1, keep, recv, pair, extra, kept, sent_y, sent_z, extra_out):
+    per = keep.shape[0] // 3
     half = per // 2
-    more = extra[...] + get_pair(recv, size, extra.shape[0])
+    rows = extra.shape[0]
+    more = extra[...] + get_pair(pair, 0, rows)
     extra_out[...] = more
-    put_pair(sent_y, 4 * half, more)
-    low, high = bit0[0], bit1[0]
+    high = more.astype(BF16).astype(F32)
+    term = jnp.where(pl.program_id(0) == 0, high, more - high)
+    sent_y[2 * half, :rows] = term.astype(BF16)
+    low, far = bit0[0], bit1[0]
 
     def total(i):
         return (keep[i].astype(F32) + recv[i].astype(F32)).astype(BF16)
 
-    for k in range(2):
-        for section in range(3):
-            base = (k * 3 + section) * per
-            for e in range(half):
-                if section < 2:
-                    mine, other = base + 2 * e + low, base + 2 * e + 1 - low
-                    dest, at = sent_y, (k * 2 + section) * half + e
-                else:
-                    first = base + 4 * (e // 2) + e % 2
-                    mine, other = first + 2 * high, first + 2 * (1 - high)
-                    dest, at = sent_z, k * half + e
-                kept[base // 2 + e] = total(mine)
-                dest[at] = total(other)
+    for section in range(3):
+        base = section * per
+        for e in range(half):
+            if section < 2:
+                mine, other = base + 2 * e + low, base + 2 * e + 1 - low
+                dest, at = sent_y, section * half + e
+            else:
+                first = base + 4 * (e // 2) + e % 2
+                mine, other = first + 2 * far, first + 2 * (1 - far)
+                dest, at = sent_z, e
+            kept[section * half + e] = total(mine)
+            dest[at] = total(other)
+
+
+def split(bits, keep, recv, extra, name):
+    size, rows, lanes = keep.shape
+    half = size // 12
+    smem = pl.BlockSpec(memory_space=pltpu.SMEM)
+    step = lambda n: pl.BlockSpec((n, rows, lanes), lambda k: (k, 0, 0))
+    whole = pl.BlockSpec(extra.shape, lambda k: (0, 0))
+    sizes = [3 * half, 2 * half + 1, half]
+    return pl.pallas_call(
+        split_kernel,
+        grid=(2,),
+        in_specs=[
+            smem,
+            smem,
+            step(size // 2),
+            step(size // 2),
+            pl.BlockSpec((2, rows, lanes), lambda k: (size // 2, 0, 0)),
+            whole,
+        ],
+        out_specs=[step(n) for n in sizes] + [whole],
+        out_shape=[jax.ShapeDtypeStruct((2 * n, rows, lanes), BF16) for n in sizes]
+        + [jax.ShapeDtypeStruct(extra.shape, F32)],
+        cost_estimate=COST(1.0),
+        compiler_params=pltpu.CompilerParams(vmem_limit_bytes=VMEM_LIMIT),
+        name=name,
+    )(*bits, keep, recv, recv, extra)
 
 
 def join_kernel(keep, recv_y, recv_z, extra, kept, sent, extra_out):
     half = keep.shape[0] // 6
-    more = extra[...] + get_pair(recv_y, 4 * half, extra.shape[0])
+    rows, part = extra.shape[0], 2 * half + 1
+    terms = [recv_y[k * part + 2 * half, :rows].astype(F32) for k in range(2)]
+    more = extra[...] + (terms[0] + terms[1])
     extra_out[...] = more
     put_pair(sent, 3 * half, more)
     for k in range(2):
         for section in range(3):
             for e in range(half):
                 if section < 2:
-                    other = recv_y[(k * 2 + section) * half + e]
+                    other = recv_y[k * part + section * half + e]
                 else:
                     other = recv_z[k * half + e]
                 value = keep[(k * 3 + section) * half + e].astype(F32) + other.astype(F32)
@@ -1179,9 +1209,7 @@
         keep = keep.reshape(size, rows, model)
 
         bits = [parity, digit(dp, 1)]
-        keep, send_y, send_z, vec = combine(
-            split_kernel, bits, [keep, recv, vec], [24, 18, 8], "combine0"
-        )
+        keep, send_y, send_z, vec = split(bits, keep, recv, vec, "combine0")
         recv_y, recv_z = swap(send_y, "dp", 1), swap(send_z, "dp", 2)
         x, keep = bar((hidden_in, keep))
         carry = backward(0, 5, x, None, 0)

time: 167 us -> 166 us (level)
    pallas_call x2 -> x1, Pallas kernels: 5.94 us -> 2.5 us  [combine(): pl.pallas_call(kernel, in_specs=[pl.BlockSpec(memory_space=pltpu.SMEM)] *...]
    pallas_call x0 -> x1, Pallas kernels: none -> 3.07 us  [split(): pl.pallas_call(split_kernel, grid=(2,), in_specs=[smem, smem, step(size /...]
  transfers between devices with their start and end apart: 24 -> 24, of which waited for: 10 -> 10; matrix products, arithmetic and copies ran while one was open for 0% -> 0% of each run, Pallas kernels for 66% -> 65%
where the time goes in v3:
time: 166 us
  Pallas kernels  112 us (67%)
  waiting for transfers between devices  27.5 us (17%)
  starting transfers between devices  23.3 us (14%)
  local copies, waits for them, and re-layouts  1.82 us (1%)
    pallas_call x2, Pallas kernels, mid(): pl.pallas_call(functools.partial(mid_kernel, half, width, blocks), grid_s...  49.1 us
    pallas_call x2, Pallas kernels, attn_bwd(): pl.pallas_call(functools.partial(attn_bwd_kernel, first, count, heads, sh...  27.7 us
    ppermute x24, waiting for transfers between devices, swap(): return lax.ppermute(value, axis, [(i, i ^ bit) for i in range(count)])  27.5 us
    ppermute x24, starting transfers between devices, swap(): return lax.ppermute(value, axis, [(i, i ^ bit) for i in range(count)])  23.3 us
    pallas_call x1, Pallas kernels, attn_fwd(): pl.pallas_call(functools.partial(attn_fwd_kernel, heads, short_blocks), g...  15.2 us
    pallas_call x1, Pallas kernels, prep(): pl.pallas_call(prep_kernel, in_specs=[vmem] * 10, out_specs=[vmem] * len(...  9.36 us
  transfers between devices with their start and end apart: 24, of which 10 were waited for; matrix products, arithmetic and copies ran while one was open for 0% of the time, Pallas kernels for 65%

profile of v3, /device:TPU:0, one launch (start us, length us, event | category | flops | bytes accessed | tf_op | source)
XLA Modules:
  0.0 165.9 jit_solution(10538459406616420465)
XLA Ops:
  0.6 2.1 %pack.1.w0 = bf16[592,768]{1,0:T(8,128)(2,1)} custom-call(bf16[192,768]{1,0:T(8,128)(2,1)} %ow.1, bf16[192,768]{1,0:T(8,128)(2,1)} %up.1, bf16[192,768]{1,0:T(8,128)(2,1)} %dn.1, f32[768]{0:T(1024)} %ub.1), custom_call_target="tpu_custom_call" | custom-call | flops 1000000000 | bytes 1000000 | tf_op jit(solution)/shard_map/pack/pallas_call | solution.py:1087
  2.8 3.0 %collective-permute-start = (bf16[592,768]{1,0:T(8,128)(2,1)}, bf16[592,768]{1,0:T(8,128)(2,1)}, u32[]{:S(2)}, u32[]{:S(2)}) collective-permute-start(bf16[592,768]{1,0:T(8,128)(2,1)} %pack.1.w0), channel_id=1, source_target_pairs={{0,2},{1,3},{2,0},{3,1},{4,6},{5,7},{6,4},{7,5},{8,10},{9,11},{10,... | collective-permute-start | bytes 2727944 | tf_op jit(solution)/shard_map/ppermute | solution.py:1031
  5.7 15.2 %attn_fwd.1 = (bf16[8,576,512]{2,1,0:T(8,128)(2,1)}, bf16[1,192,512]{2,1,0:T(8,128)(2,1)}, bf16[2,192,512]{2,1,0:T(8,128)(2,1)}, bf16[2,192,512]{2,1,0:T(8,128)(...) custom-call(s32[1]{0:T(128)} %bitcast.me.refs_0_, ...), custom_call_target="tpu_custom_call" | custom-call | flops 16000000000 | bytes 16000000 | tf_op jit(solution)/shard_map/attn_fwd/pallas_call | solution.py:147
  21.0 5.2 %collective-permute-done.w2 = bf16[592,768]{1,0:T(8,128)(2,1)} collective-permute-done((bf16[592,768]{1,0:T(8,128)(2,1)}, bf16[592,768]{1,0:T(8,128)(2,1)}, u32[]{:S(2)}, u32[]{:S(2)}) %collective-permute-start) | collective-permute-done | bytes 909344 | tf_op jit(solution)/shard_map/ppermute | solution.py:1031
  26.7 1.7 %collective-permute-start.3 = (bf16[2,192,512]{2,1,0:T(8,128)(2,1)}, bf16[2,192,512]{2,1,0:T(8,128)(2,1)}, u32[]{:S(2)}, u32[]{:S(2)}) collective-permute-start(bf16[2,192,512]{2,1,0:T(8,128)(2,1)} %get-tuple-element.149), channel_id=1, source_target_pairs={{0,2},{1,3},{2,0},{3,1},{4,6},{5,7},{6,4},{7,5},{8,10},{9,11},{10,... | collective-permute-start | bytes 1179656 | tf_op jit(solution)/shard_map/ppermute | solution.py:1031
  29.0 1.7 %collective-permute-start.7 = (bf16[2,192,512]{2,1,0:T(8,128)(2,1)}, bf16[2,192,512]{2,1,0:T(8,128)(2,1)}, u32[]{:S(2)}, u32[]{:S(2)}) collective-permute-start(bf16[2,192,512]{2,1,0:T(8,128)(2,1)} %get-tuple-element.172), channel_id=1, source_target_pairs={{0,2},{1,3},{2,0},{3,1},{4,6},{5,7},{6,4},{7,5},{8,10},{9,11},{10,... | collective-permute-start | bytes 1179656 | tf_op jit(solution)/shard_map/ppermute | solution.py:1031
  30.8 9.4 %prep.1 = (bf16[768,768]{1,0:T(8,128)(2,1)}, bf16[4,768,192]{2,1,0:T(8,128)(2,1)}, bf16[4,768,192]{2,1,0:T(8,128)(2,1)}, bf16[4,192,768]{2,1,0:T(8,128)(2,1)}, b...) custom-call(bf16[592,768]{1,0:T(8,128)(2,1)} %pack.1.w0, ...), custom_call_target="tpu_custom_call" | custom-call | flops 4000000000 | bytes 4000000 | tf_op jit(solution)/shard_map/prep/pallas_call | solution.py:432
  40.2 6.5 %collective-permute-done.4.refs_3_.refs_7_ = bf16[2,192,512]{2,1,0:T(8,128)(2,1)} collective-permute-done((bf16[2,192,512]{2,1,0:T(8,128)(2,1)}, bf16[2,192,512]{2,1,0:T(8,128)(2,1)}, u32[]{:S(2)}, u32[]{:S(2)}) %collective-permute-start.4) | collective-permute-done | bytes 393248 | tf_op jit(solution)/shard_map/ppermute | solution.py:1031
  46.7 23.4 %mid0.1 = (bf16[1024,768]{1,0:T(8,128)(2,1)}, bf16[2,192,512]{2,1,0:T(8,128)(2,1)}, bf16[2,192,512]{2,1,0:T(8,128)(2,1)}, bf16[2,192,512]{2,1,0:T(8,128)(2,1)}, ...) custom-call(s32[1]{0:T(128)} %bitcast.me.refs_0_, ...), custom_call_target="tpu_custom_call" | custom-call | flops 24999999488 | bytes 25000000 | tf_op jit(solution)/shard_map/mid0/pallas_call | solution.py:723
  70.8 1.4 collective-permute-start.11
  72.4 25.7 %mid1.1 = (bf16[1024,768]{1,0:T(8,128)(2,1)}, bf16[2,192,512]{2,1,0:T(8,128)(2,1)}, bf16[2,192,512]{2,1,0:T(8,128)(2,1)}, bf16[2,192,512]{2,1,0:T(8,128)(2,1)}, ...) custom-call(s32[1]{0:T(128)} %bitcast.me.refs_0_, ...), custom_call_target="tpu_custom_call", output_to_operand_aliasing={{0}: (22, {})} | custom-call | flops 24999999488 | bytes 25000000 | tf_op jit(solution)/shard_map/mid1/pallas_call | solution.py:723
  98.7 1.6 collective-permute-start.16
  100.4 1.9 %collective-permute-done.12 = bf16[1200,768]{1,0:T(8,128)(2,1)} collective-permute-done((bf16[1200,768]{1,0:T(8,128)(2,1)}, bf16[1200,768]{1,0:T(8,128)(2,1)}, u32[]{:S(2)}, u32[]{:S(2)}) %collective-permute-start.12) | collective-permute-done | bytes 1843232 | tf_op jit(solution)/shard_map/ppermute | solution.py:1031
  102.3 3.1 %combine0.1 = (bf16[24,24,768]{2,1,0:T(8,128)(2,1)}, bf16[18,24,768]{2,1,0:T(8,128)(2,1)}, bf16[8,24,768]{2,1,0:T(8,128)(2,1)}, f32[16,768]{1,0:T(8,128)}) custom-call(s32[1]{0:T(128)} %bitcast.2.bit0.refs_1_.refs_0_, s32[1]{0:T(128)} %bitcast.3.bit1.refs_1_.refs_0_, bf16[48,24,768]{2,1,0:T(8,128)(2,1)} %bitcast.12, bf16[50,24,768]{2,1,0:T(8,128)(2,1)} %bitcast.5.recv.pair, ...), custom_call_target="tpu_custom_call" | custom-call | flops 1000000000 | bytes 1000000 | tf_op jit(solution)/shard_map/combine0/pallas_call | solution.py:787
  105.4 1.7 %collective-permute-start.13 = (bf16[18,24,768]{2,1,0:T(8,128)(2,1)}, bf16[18,24,768]{2,1,0:T(8,128)(2,1)}, u32[]{:S(2)}, u32[]{:S(2)}) collective-permute-start(bf16[18,24,768]{2,1,0:T(8,128)(2,1)} %get-tuple-element.201), channel_id=1, source_target_pairs={{0,4},{4,0},{8,12},{12,8},{16,20},{20,16},{24,28},{28,24},{1,5},{5... | collective-permute-start | bytes 1990664 | tf_op jit(solution)/shard_map/ppermute | solution.py:1031
  107.1 1.6 collective-permute-start.14
  108.6 15.9 %attn_bwd0.1 = (f32[192,4096]{1,0:T(8,128)}, f32[576,192]{1,0:T(8,128)}, f32[8,576]{1,0:T(8,128)}) custom-call(s32[1]{0:T(128)} %bitcast.me.refs_0_, s32[1]{0:T(128)} %bitcast.2.bit0.refs_1_.refs_0_, s32[16]{0:T(128)} %refs_2_.5, s32[4]{0:T(128)} %refs_3_.5, bf16[192,4096]{1,0:T(8,128)(2,1)} %refs_4_.7, bf16[192,576]{1,0:T(8,128)(2,1)} %bitcast.14, ...), custom_call_target="tpu_custom_call" | custom-call | flops 20000000000 | bytes 20000000 | tf_op jit(solution)/shard_map/attn_bwd0/pallas_call | solution.py:351
  124.5 2.5 %combine1.1 = (bf16[12,24,768]{2,1,0:T(8,128)(2,1)}, bf16[14,24,768]{2,1,0:T(8,128)(2,1)}, f32[16,768]{1,0:T(8,128)}) custom-call(bf16[24,24,768]{2,1,0:T(8,128)(2,1)} %get-tuple-element.200.keep, bf16[18,24,768]{2,1,0:T(8,128)(2,1)} %collective-permute-done.13.recv_y, bf16[8,24,768]{2,1,0:T(8,128)(2,1)} %collective-permute-done.14.recv_z, ...), custom_call_target="tpu_custom_call" | custom-call | flops 1000000000 | bytes 1000000 | tf_op jit(solution)/shard_map/combine1/pallas_call | solution.py:851
  127.0 2.9 %collective-permute-start.18 = (bf16[14,24,768]{2,1,0:T(8,128)(2,1)}, bf16[14,24,768]{2,1,0:T(8,128)(2,1)}, u32[]{:S(2)}, u32[]{:S(2)}) collective-permute-start(bf16[14,24,768]{2,1,0:T(8,128)(2,1)} %get-tuple-element.225), channel_id=1, source_target_pairs={{0,2},{1,3},{2,0},{3,1},{4,6},{5,7},{6,4},{7,5},{8,10},{9,11},{10,... | collective-permute-start | bytes 1548296 | tf_op jit(solution)/shard_map/ppermute | solution.py:1031
  129.9 11.8 %attn_bwd5.1 = (f32[192,4096]{1,0:T(8,128)}, bf16[4,72,192]{2,1,0:T(8,128)(2,1)}, bf16[5,72,192]{2,1,0:T(8,128)(2,1)}, f32[24,192]{1,0:T(8,128)}) custom-call(s32[1]{0:T(128)} %bitcast.me.refs_0_, s32[1]{0:T(128)} %bitcast.2.bit0.refs_1_.refs_0_, s32[16]{0:T(128)} %refs_2_.5, s32[4]{0:T(128)} %refs_3_.5, ...), custom_call_target="tpu_custom_call", output_to_operand_aliasing={{0}: (13, {})} | custom-call | flops 12000000000 | bytes 12000000 | tf_op jit(solution)/shard_map/attn_bwd5/pallas_call | solution.py:351
  146.2 1.9 %collective-permute-done.19.refs_3_ = bf16[5,72,192]{2,1,0:T(8,128)(2,1)S(1)} collective-permute-done((bf16[5,72,192]{2,1,0:T(8,128)(2,1)}, bf16[5,72,192]{2,1,0:T(8,128)(2,1)S(1)}, u32[]{:S(2)}, u32[]{:S(2)}) %collective-permute-start.19) | collective-permute-done | bytes 138272 | tf_op jit(solution)/shard_map/ppermute | solution.py:1031
  149.7 3.5 %collective-permute-done.21.refs_0_ = bf16[2,24,768]{2,1,0:T(8,128)(2,1)S(1)} collective-permute-done((bf16[2,24,768]{2,1,0:T(8,128)(2,1)S(1)}, bf16[2,24,768]{2,1,0:T(8,128)(2,1)S(1)}, u32[]{:S(2)}, u32[]{:S(2)}) %collective-permute-start.21) | collective-permute-done | bytes 73760 | tf_op jit(solution)/shard_map/ppermute | solution.py:1031
  154.6 2.9 %collective-permute-start.23 = (bf16[5,24,768]{2,1,0:T(8,128)(2,1)S(1)}, bf16[5,24,768]{2,1,0:T(8,128)(2,1)S(1)}, u32[]{:S(2)}, u32[]{:S(2)}) collective-permute-start(bf16[5,24,768]{2,1,0:T(8,128)(2,1)S(1)} %get-tuple-element.247), channel_id=1, source_target_pairs={{0,16},{4,20},{8,24},{12,28},{16,0},{20,4},{24,8},{28,12},{1,17},{... | collective-permute-start | bytes 552968 | tf_op jit(solution)/shard_map/ppermute | solution.py:1031
  157.6 6.7 %collective-permute-done.23.wr = bf16[5,24,768]{2,1,0:T(8,128)(2,1)S(1)} collective-permute-done((bf16[5,24,768]{2,1,0:T(8,128)(2,1)S(1)}, bf16[5,24,768]{2,1,0:T(8,128)(2,1)S(1)}, u32[]{:S(2)}, u32[]{:S(2)}) %collective-permute-start.23) | collective-permute-done | bytes 184352 | tf_op jit(solution)/shard_map/ppermute | solution.py:1031
  (46 shorter events, 11.6 us)
Async XLA Ops:
  2.8 23.5 %collective-permute-start = (bf16[592,768]{1,0:T(8,128)(2,1)}, bf16[592,768]{1,0:T(8,128)(2,1)}, u32[]{:S(2)}, u32[]{:S(2)}) collective-permute-start(bf16[592,768]{1,0:T(8,128)(2,1)} %pack.1.w0), channel_id=1, source_target_pairs={{0,2},{1,3},{2,0},{3,1},{4,6},{5,7},{6,4},{7,5},{8,10},{9,11},{10,... | collective-permute-start | bytes 2727944 | tf_op jit(solution)/shard_map/ppermute | solution.py:1031
  5.7 20.5 %collective-permute-start.1 = (bf16[592,768]{1,0:T(8,128)(2,1)}, bf16[592,768]{1,0:T(8,128)(2,1)}, u32[]{:S(2)}, u32[]{:S(2)}) collective-permute-start(bf16[592,768]{1,0:T(8,128)(2,1)} %pack.1.w0), channel_id=1, source_target_pairs={{0,1},{1,0},{2,3},{3,2},{4,5},{5,4},{6,7},{7,6},{8,9},{9,8},{10,11... | collective-permute-start | bytes 2727944 | tf_op jit(solution)/shard_map/ppermute | solution.py:1031
  26.2 2.8 %collective-permute-start.5 = (bf16[592,768]{1,0:T(8,128)(2,1)}, bf16[592,768]{1,0:T(8,128)(2,1)}, u32[]{:S(2)}, u32[]{:S(2)}) collective-permute-start(bf16[592,768]{1,0:T(8,128)(2,1)} %collective-permute-done.w2), channel_id=1, source_target_pairs={{0,1},{1,0},{2,3},{3,2},{4,5},{5,4},{6,7},{7,6},{8,9},{9,8},{10,11... | collective-permute-start | bytes 2727944 | tf_op jit(solution)/shard_map/ppermute | solution.py:1031
  26.2 13.9 %collective-permute-start.2 = (bf16[2,192,512]{2,1,0:T(8,128)(2,1)}, bf16[2,192,512]{2,1,0:T(8,128)(2,1)}, u32[]{:S(2)}, u32[]{:S(2)}) collective-permute-start(bf16[2,192,512]{2,1,0:T(8,128)(2,1)} %get-tuple-element.148), channel_id=1, source_target_pairs={{0,1},{1,0},{2,3},{3,2},{4,5},{5,4},{6,7},{7,6},{8,9},{9,8},{10,11... | collective-permute-start | bytes 1179656 | tf_op jit(solution)/shard_map/ppermute | solution.py:1031
  26.7 13.5 %collective-permute-start.3 = (bf16[2,192,512]{2,1,0:T(8,128)(2,1)}, bf16[2,192,512]{2,1,0:T(8,128)(2,1)}, u32[]{:S(2)}, u32[]{:S(2)}) collective-permute-start(bf16[2,192,512]{2,1,0:T(8,128)(2,1)} %get-tuple-element.149), channel_id=1, source_target_pairs={{0,2},{1,3},{2,0},{3,1},{4,6},{5,7},{6,4},{7,5},{8,10},{9,11},{10,... | collective-permute-start | bytes 1179656 | tf_op jit(solution)/shard_map/ppermute | solution.py:1031
  28.5 18.2 %collective-permute-start.4 = (bf16[2,192,512]{2,1,0:T(8,128)(2,1)}, bf16[2,192,512]{2,1,0:T(8,128)(2,1)}, u32[]{:S(2)}, u32[]{:S(2)}) collective-permute-start(bf16[2,192,512]{2,1,0:T(8,128)(2,1)} %get-tuple-element.150), channel_id=1, source_target_pairs={{0,3},{1,2},{2,1},{3,0},{4,7},{5,6},{6,5},{7,4},{8,11},{9,10},{10,... | collective-permute-start | bytes 1179656 | tf_op jit(solution)/shard_map/ppermute | solution.py:1031
  28.5 41.6 %collective-permute-start.6 = (bf16[2,192,512]{2,1,0:T(8,128)(2,1)}, bf16[2,192,512]{2,1,0:T(8,128)(2,1)}, u32[]{:S(2)}, u32[]{:S(2)}) collective-permute-start(bf16[2,192,512]{2,1,0:T(8,128)(2,1)} %get-tuple-element.171), channel_id=1, source_target_pairs={{0,1},{1,0},{2,3},{3,2},{4,5},{5,4},{6,7},{7,6},{8,9},{9,8},{10,11... | collective-permute-start | bytes 1179656 | tf_op jit(solution)/shard_map/ppermute | solution.py:1031
  29.0 41.1 %collective-permute-start.7 = (bf16[2,192,512]{2,1,0:T(8,128)(2,1)}, bf16[2,192,512]{2,1,0:T(8,128)(2,1)}, u32[]{:S(2)}, u32[]{:S(2)}) collective-permute-start(bf16[2,192,512]{2,1,0:T(8,128)(2,1)} %get-tuple-element.172), channel_id=1, source_target_pairs={{0,2},{1,3},{2,0},{3,1},{4,6},{5,7},{6,4},{7,5},{8,10},{9,11},{10,... | collective-permute-start | bytes 1179656 | tf_op jit(solution)/shard_map/ppermute | solution.py:1031
  40.2 30.0 %collective-permute-start.8 = (bf16[2,192,512]{2,1,0:T(8,128)(2,1)}, bf16[2,192,512]{2,1,0:T(8,128)(2,1)}, u32[]{:S(2)}, u32[]{:S(2)}) collective-permute-start(bf16[2,192,512]{2,1,0:T(8,128)(2,1)} %get-tuple-element.173), channel_id=1, source_target_pairs={{0,3},{1,2},{2,1},{3,0},{4,7},{5,6},{6,5},{7,4},{8,11},{9,10},{10,... | collective-permute-start | bytes 1179656 | tf_op jit(solution)/shard_map/ppermute | solution.py:1031
  70.1 27.9 %collective-permute-start.10 = (bf16[2,192,512]{2,1,0:T(8,128)(2,1)}, bf16[2,192,512]{2,1,0:T(8,128)(2,1)}, u32[]{:S(2)}, u32[]{:S(2)}) collective-permute-start(bf16[2,192,512]{2,1,0:T(8,128)(2,1)} %get-tuple-element.193), channel_id=1, source_target_pairs={{0,2},{1,3},{2,0},{3,1},{4,6},{5,7},{6,4},{7,5},{8,10},{9,11},{10,... | collective-permute-start | bytes 1179656 | tf_op jit(solution)/shard_map/ppermute | solution.py:1031
  70.8 27.3 %collective-permute-start.11 = (bf16[2,192,512]{2,1,0:T(8,128)(2,1)}, bf16[2,192,512]{2,1,0:T(8,128)(2,1)}, u32[]{:S(2)}, u32[]{:S(2)}) collective-permute-start(bf16[2,192,512]{2,1,0:T(8,128)(2,1)} %get-tuple-element.194), channel_id=1, source_target_pairs={{0,3},{1,2},{2,1},{3,0},{4,7},{5,6},{6,5},{7,4},{8,11},{9,10},{10,... | collective-permute-start | bytes 1179656 | tf_op jit(solution)/shard_map/ppermute | solution.py:1031
  72.2 25.9 %collective-permute-start.9 = (bf16[2,192,512]{2,1,0:T(8,128)(2,1)}, bf16[2,192,512]{2,1,0:T(8,128)(2,1)}, u32[]{:S(2)}, u32[]{:S(2)}) collective-permute-start(bf16[2,192,512]{2,1,0:T(8,128)(2,1)} %get-tuple-element.192), channel_id=1, source_target_pairs={{0,1},{1,0},{2,3},{3,2},{4,5},{5,4},{6,7},{7,6},{8,9},{9,8},{10,11... | collective-permute-start | bytes 1179656 | tf_op jit(solution)/shard_map/ppermute | solution.py:1031
  98.1 4.2 %collective-permute-start.12 = (bf16[1200,768]{1,0:T(8,128)(2,1)}, bf16[1200,768]{1,0:T(8,128)(2,1)}, u32[]{:S(2)}, u32[]{:S(2)}) collective-permute-start(bf16[1200,768]{1,0:T(8,128)(2,1)} %get-tuple-element.196), channel_id=1, source_target_pairs={{0,1},{1,0},{2,3},{3,2},{4,5},{5,4},{6,7},{7,6},{8,9},{9,8},{10,11... | collective-permute-start | bytes 5529608 | tf_op jit(solution)/shard_map/ppermute | solution.py:1031
  98.5 31.4 %collective-permute-start.15 = (bf16[2,192,512]{2,1,0:T(8,128)(2,1)}, bf16[2,192,512]{2,1,0:T(8,128)(2,1)}, u32[]{:S(2)}, u32[]{:S(2)}) collective-permute-start(bf16[2,192,512]{2,1,0:T(8,128)(2,1)} %get-tuple-element.218), channel_id=1, source_target_pairs={{0,1},{1,0},{2,3},{3,2},{4,5},{5,4},{6,7},{7,6},{8,9},{9,8},{10,11... | collective-permute-start | bytes 1179656 | tf_op jit(solution)/shard_map/ppermute | solution.py:1031
  98.7 31.2 %collective-permute-start.16 = (bf16[2,192,512]{2,1,0:T(8,128)(2,1)}, bf16[2,192,512]{2,1,0:T(8,128)(2,1)}, u32[]{:S(2)}, u32[]{:S(2)}) collective-permute-start(bf16[2,192,512]{2,1,0:T(8,128)(2,1)} %get-tuple-element.219), channel_id=1, source_target_pairs={{0,2},{1,3},{2,0},{3,1},{4,6},{5,7},{6,4},{7,5},{8,10},{9,11},{10,... | collective-permute-start | bytes 1179656 | tf_op jit(solution)/shard_map/ppermute | solution.py:1031
  100.3 29.6 %collective-permute-start.17 = (bf16[2,192,512]{2,1,0:T(8,128)(2,1)}, bf16[2,192,512]{2,1,0:T(8,128)(2,1)}, u32[]{:S(2)}, u32[]{:S(2)}) collective-permute-start(bf16[2,192,512]{2,1,0:T(8,128)(2,1)} %get-tuple-element.220), channel_id=1, source_target_pairs={{0,3},{1,2},{2,1},{3,0},{4,7},{5,6},{6,5},{7,4},{8,11},{9,10},{10,... | collective-permute-start | bytes 1179656 | tf_op jit(solution)/shard_map/ppermute | solution.py:1031
  105.4 19.1 %collective-permute-start.13 = (bf16[18,24,768]{2,1,0:T(8,128)(2,1)}, bf16[18,24,768]{2,1,0:T(8,128)(2,1)}, u32[]{:S(2)}, u32[]{:S(2)}) collective-permute-start(bf16[18,24,768]{2,1,0:T(8,128)(2,1)} %get-tuple-element.201), channel_id=1, source_target_pairs={{0,4},{4,0},{8,12},{12,8},{16,20},{20,16},{24,28},{28,24},{1,5},{5... | collective-permute-start | bytes 1990664 | tf_op jit(solution)/shard_map/ppermute | solution.py:1031
  107.1 17.4 %collective-permute-start.14 = (bf16[8,24,768]{2,1,0:T(8,128)(2,1)}, bf16[8,24,768]{2,1,0:T(8,128)(2,1)}, u32[]{:S(2)}, u32[]{:S(2)}) collective-permute-start(bf16[8,24,768]{2,1,0:T(8,128)(2,1)} %get-tuple-element.202), channel_id=1, source_target_pairs={{0,8},{4,12},{8,0},{12,4},{16,24},{20,28},{24,16},{28,20},{1,9},{5... | collective-permute-start | bytes 884744 | tf_op jit(solution)/shard_map/ppermute | solution.py:1031
  127.0 14.9 %collective-permute-start.18 = (bf16[14,24,768]{2,1,0:T(8,128)(2,1)}, bf16[14,24,768]{2,1,0:T(8,128)(2,1)}, u32[]{:S(2)}, u32[]{:S(2)}) collective-permute-start(bf16[14,24,768]{2,1,0:T(8,128)(2,1)} %get-tuple-element.225), channel_id=1, source_target_pairs={{0,2},{1,3},{2,0},{3,1},{4,6},{5,7},{6,4},{7,5},{8,10},{9,11},{10,... | collective-permute-start | bytes 1548296 | tf_op jit(solution)/shard_map/ppermute | solution.py:1031
  141.9 6.1 %collective-permute-start.19 = (bf16[5,72,192]{2,1,0:T(8,128)(2,1)}, bf16[5,72,192]{2,1,0:T(8,128)(2,1)S(1)}, u32[]{:S(2)}, u32[]{:S(2)}) collective-permute-start(bf16[5,72,192]{2,1,0:T(8,128)(2,1)} %get-tuple-element.228), channel_id=1, source_target_pairs={{0,4},{4,0},{8,12},{12,8},{16,20},{20,16},{24,28},{28,24},{1,5},{5... | collective-permute-start | bytes 414728 | tf_op jit(solution)/shard_map/ppermute | solution.py:1031
  145.7 7.7 %collective-permute-start.20 = (bf16[6,24,768]{2,1,0:T(8,128)(2,1)S(1)}, bf16[6,24,768]{2,1,0:T(8,128)(2,1)S(1)}, u32[]{:S(2)}, u32[]{:S(2)}) collective-permute-start(bf16[6,24,768]{2,1,0:T(8,128)(2,1)S(1)} %get-tuple-element.234), channel_id=1, source_target_pairs={{0,8},{4,12},{8,0},{12,4},{16,24},{20,28},{24,16},{28,20},{1,9},{5... | collective-permute-start | bytes 663560 | tf_op jit(solution)/shard_map/ppermute | solution.py:1031
  148.3 6.2 %collective-permute-start.22 = (bf16[3,72,192]{2,1,0:T(8,128)(2,1)S(1)}, bf16[3,72,192]{2,1,0:T(8,128)(2,1)S(1)}, u32[]{:S(2)}, u32[]{:S(2)}) collective-permute-start(bf16[3,72,192]{2,1,0:T(8,128)(2,1)S(1)} %get-tuple-element.244), channel_id=1, source_target_pairs={{0,8},{4,12},{8,0},{12,4},{16,24},{20,28},{24,16},{28,20},{1,9},{5... | collective-permute-start | bytes 248840 | tf_op jit(solution)/shard_map/ppermute | solution.py:1031
  148.9 4.4 %collective-permute-start.21 = (bf16[2,24,768]{2,1,0:T(8,128)(2,1)S(1)}, bf16[2,24,768]{2,1,0:T(8,128)(2,1)S(1)}, u32[]{:S(2)}, u32[]{:S(2)}) collective-permute-start(bf16[2,24,768]{2,1,0:T(8,128)(2,1)S(1)} %get-tuple-element.235), channel_id=1, source_target_pairs={{0,4},{4,0},{8,12},{12,8},{16,20},{20,16},{24,28},{28,24},{1,5},{5... | collective-permute-start | bytes 221192 | tf_op jit(solution)/shard_map/ppermute | solution.py:1031
  154.6 9.6 %collective-permute-start.23 = (bf16[5,24,768]{2,1,0:T(8,128)(2,1)S(1)}, bf16[5,24,768]{2,1,0:T(8,128)(2,1)S(1)}, u32[]{:S(2)}, u32[]{:S(2)}) collective-permute-start(bf16[5,24,768]{2,1,0:T(8,128)(2,1)S(1)} %get-tuple-element.247), channel_id=1, source_target_pairs={{0,16},{4,20},{8,24},{12,28},{16,0},{20,4},{24,8},{28,12},{1,17},{... | collective-permute-start | bytes 552968 | tf_op jit(solution)/shard_map/ppermute | solution.py:1031
  (4 other events, 9.4 us)
